TPU v7x, 32 devices: a whole 2x2x4 slice. The times are simulated.
32 devices in a mesh: groups: 2 (over y), ctx: 4 (over x, core), head: 4 (over z).
Axes of the slice: x: 2, y: 2, z: 4, core: 2. Of those that a mesh axis runs over, the one named last changes fastest.
Arguments:
- queries: bfloat16 [1536, 8, 5, 128], P(('groups', 'ctx'), 'head'), parts along dimension 0, may hold values from -6 to 6
- keys_values: bfloat16 [1536, 8, 2, 128], P(('groups', 'ctx'), 'head'), parts along dimension 0, may hold values from -6 to 6
- prior_state: bfloat16 [16, 8256, 128], P(('groups', 'head'), 'ctx'), parts along dimension 0, may hold values from -224 to 224
- counts: int32 [2], P('groups'), parts along dimension 0, may hold values from 384 to 1535
- continuation: int32 [64], P('groups'), parts along dimension 0, may hold values from 0 to 75967
- query_table: bfloat16 [75968, 8, 5, 128], P('ctx', 'head'), may hold values from -6 to 6
- pair_table: bfloat16 [75968, 8, 2, 128], P('ctx', 'head'), may hold values from -6 to 6
Outputs:
- readout: bfloat16 [1536, 8, 5, 128], P(('groups', 'ctx'), 'head'), parts along dimension 0
- decode_out: bfloat16 [64, 8, 5, 128], P(('groups', 'ctx'), 'head'), parts along dimension 0
- decode_state: float32 [16, 8256, 128], P(('groups', 'head'), 'ctx'), parts along dimension 0
There are 2 independent parts, one for each index of `groups`. A program takes and returns all parts, laid end to end along the dimension named above; an argument that names none is the same for every part. Nothing has to cross between parts.
All inputs are finite; a program needn't handle non-finite values.
Results may differ from a plain program's by a relative error of at most 0.0048.
The roundings to bfloat16 on the way count: a program that leaves them out, or rounds other values in their place, can miss the bound.
Values may be sent and summed in bfloat16 or wider, within the bound.
A program may use at most 256 MiB of HBM per device.

v0:
```python
import functools

import jax
import jax.numpy as jnp
from jax import lax
from jax.experimental import pallas as pl
from jax.experimental.pallas import tpu as pltpu
from jax.sharding import PartitionSpec as P

ROOT_TWO = 2.0**0.5
MESH = pl.DeviceIdType.MESH
TILE = 256
LANES = 128


def round_up(number, multiple):
    return (number + multiple - 1) // multiple * multiple


def pick_kernel(ids_ref, query_table, pair_table, query_out, pair_out, query_sem, pair_sem):
    vocab_rows = query_table.shape[0]
    first_row = lax.axis_index("ctx") * vocab_rows
    query_out[...] = jnp.zeros_like(query_out)
    pair_out[...] = jnp.zeros_like(pair_out)

    def each(step, act):
        row = ids_ref[step] - first_row

        @pl.when(jnp.logical_and(row >= 0, row < vocab_rows))
        def _():
            act(pltpu.make_async_copy(query_table.at[row], query_out.at[step], query_sem.at[step]))
            act(pltpu.make_async_copy(pair_table.at[row], pair_out.at[step], pair_sem.at[step]))

    for step in range(query_out.shape[0]):
        each(step, lambda copy: copy.start())
    for step in range(query_out.shape[0]):
        each(step, lambda copy: copy.wait())


def pick_rows(ids, query_table, pair_table):
    steps = ids.shape[0]
    return pl.pallas_call(
        pick_kernel,
        out_shape=(
            jax.ShapeDtypeStruct((steps,) + query_table.shape[1:], query_table.dtype),
            jax.ShapeDtypeStruct((steps,) + pair_table.shape[1:], pair_table.dtype),
        ),
        in_specs=[
            pl.BlockSpec(memory_space=pltpu.SMEM),
            pl.BlockSpec(memory_space=pl.ANY),
            pl.BlockSpec(memory_space=pl.ANY),
        ],
        out_specs=(
            pl.BlockSpec(memory_space=pltpu.VMEM),
            pl.BlockSpec(memory_space=pltpu.VMEM),
        ),
        scratch_shapes=[pltpu.SemaphoreType.DMA((steps,)), pltpu.SemaphoreType.DMA((steps,))],
        name="pick_rows",
    )(ids, query_table, pair_table)


def main_kernel(
    sizes,
    counts,
    queries,
    blob,
    prior,
    window_out,
    step_out,
    state_out,
    out,
    state,
    land_blob,
    land_prior,
    query_rows,
    query_plain,
    query_scaled,
    prior_turned,
    total_turned,
    step_rows,
    key_rows,
    value_rows,
    turned,
    blob_send,
    blob_recv,
    prior_send,
    prior_recv,
    local_sem,
):
    n, heads, group, tok_rows, step_count, rows_valid = sizes
    chips = n // 2
    per_shard = step_count // n
    window_rows = tok_rows * group
    window = n * tok_rows
    prior_rows = prior.shape[1]
    shifted = prior_rows == rows_valid
    state_rows = state.shape[1]
    blocks = land_prior.shape[2] // LANES
    row_tiles = out.shape[1] // TILE
    padded_keys = key_rows.shape[1]
    me = lax.axis_index("ctx")
    core = lax.rem(me, 2)
    partner = me + 1 - 2 * core

    def across(step):
        return lax.rem(me + 2 * step, n)

    def twin(index):
        return index + 1 - 2 * lax.rem(index, 2)

    barrier = pltpu.get_barrier_semaphore()
    pl.semaphore_signal(barrier, inc=1, device_id={"ctx": partner}, device_id_type=MESH)
    for step in range(1, chips):
        pl.semaphore_signal(barrier, inc=1, device_id={"ctx": across(step)}, device_id_type=MESH)
    pl.semaphore_wait(barrier, chips)

    def blob_copy(src, source, slot, target):
        return pltpu.make_async_remote_copy(
            src_ref=src,
            dst_ref=land_blob.at[source],
            send_sem=blob_send.at[slot],
            recv_sem=blob_recv.at[source],
            device_id={"ctx": target},
            device_id_type=MESH,
        )

    def landing(source):
        first = pl.multiple_of(lax.rem(source * rows_valid, LANES), 16) if shifted else 0
        return pl.ds(first, prior_rows)

    def prior_copy(src, source, head, slot, target):
        return pltpu.make_async_remote_copy(
            src_ref=src,
            dst_ref=land_prior.at[source, head, landing(source)],
            send_sem=prior_send.at[slot, head],
            recv_sem=prior_recv.at[source, head],
            device_id={"ctx": target},
            device_id_type=MESH,
        )

    def blob_own(slot):
        return blob_copy(blob, me, slot, partner if slot == 0 else across(slot))

    def blob_forward(step):
        source = across(step)
        return blob_copy(land_blob.at[source], source, chips - 1 + step, partner)

    def prior_own(slot, head):
        target = partner if slot == 0 else across(slot)
        return prior_copy(prior.at[head], me, head, slot, target)

    def prior_forward(step, head):
        source = across(step)
        return prior_copy(
            land_prior.at[source, head, landing(source)],
            source,
            head,
            chips - 1 + step,
            partner,
        )

    for slot in list(range(1, chips)) + [0]:
        blob_own(slot).start()
    for head in range(heads):
        for slot in list(range(1, chips)) + [0]:
            prior_own(slot, head).start()
    own_blob = pltpu.make_async_copy(blob, land_blob.at[me], local_sem.at[0])
    own_prior = pltpu.make_async_copy(
        prior, land_prior.at[me, :, landing(me)], local_sem.at[1]
    )
    own_blob.start()
    own_prior.start()

    if shifted:
        for source in range(n):
            lead_rows = source * rows_valid % LANES
            for first, last in (
                (0, lead_rows),
                (lead_rows + prior_rows, blocks * LANES),
            ):
                if last > first:
                    for head in range(heads):
                        land_prior[source, head, pl.ds(first, last - first), :] = jnp.zeros(
                            (last - first, LANES), jnp.bfloat16
                        )
    total_turned[...] = jnp.zeros_like(total_turned)
    for head in range(heads):
        query_rows[head, pl.ds(0, window_rows), :] = queries[head]
        query_rows[head, pl.ds(window_rows, out.shape[1] - window_rows), :] = jnp.zeros(
            (out.shape[1] - window_rows, LANES), jnp.bfloat16
        )
        spare = padded_keys - window - step_count
        if spare > 0:
            key_rows[head, pl.ds(window + step_count, spare), :] = jnp.zeros(
                (spare, LANES), jnp.bfloat16
            )
            value_rows[head, pl.ds(window + step_count, spare), :] = jnp.zeros(
                (spare, LANES), jnp.bfloat16
            )

    def place(source):
        first = source * rows_valid
        return lax.div(first, LANES), lax.rem(first, LANES)

    identity = (
        lax.broadcasted_iota(jnp.int32, (LANES, LANES), 0)
        == lax.broadcasted_iota(jnp.int32, (LANES, LANES), 1)
    ).astype(jnp.bfloat16)
    contract_last = (((1,), (1,)), ((), ()))

    def transposed(rows):
        return lax.dot_general(identity, rows, contract_last, preferred_element_type=jnp.float32)

    chunks_per_tile = TILE // LANES

    def turn_queries(head, first_tile, last_tile):
        for chunk in range(first_tile * chunks_per_tile, last_tile * chunks_per_tile):
            piece = transposed(query_rows[head, pl.ds(chunk * LANES, LANES), :])
            scaled = piece * ROOT_TWO
            query_plain[head, chunk] = piece
            query_scaled[head, chunk, pl.ds(0, LANES), :] = scaled
            query_scaled[head, chunk, pl.ds(LANES, LANES), :] = scaled

    def carry_tile(source, head, tile):
        first_offset, _ = place(source)
        columns = []
        for side in range(chunks_per_tile):
            chunk = tile * chunks_per_tile + side
            here = query_plain[head, chunk]
            pieces = []
            for block in range(blocks):
                row = lax.rem(first_offset + block, LANES)
                other = query_scaled[head, chunk, pl.ds(row, LANES), :]
                if block == 0:
                    other = jnp.where(first_offset == 0, here, other)
                pieces.append((here * other).astype(jnp.bfloat16))
            columns.append(jnp.concatenate(pieces, axis=0))
        features = jnp.concatenate(columns, axis=1)
        total_turned[head, tile] += jnp.dot(
            prior_turned[...], features, preferred_element_type=jnp.float32
        )

    def carry(source, head, first_tile, last_tile):
        prior_turned[...] = transposed(land_prior[source, head]).astype(jnp.bfloat16)

        @pl.loop(first_tile, last_tile)
        def _(tile):
            carry_tile(source, head, tile)

    full_tiles = window_rows // TILE
    own_prior.wait()
    for head in range(heads):
        turn_queries(head, 0, full_tiles)
        carry(me, head, 0, full_tiles)

    own_blob.wait()
    blob_copy(blob, partner, 0, partner).wait_recv()
    for step in range(1, chips):
        blob_copy(blob, across(step), 0, partner).wait_recv()
        blob_forward(step).start()
    for step in range(1, chips):
        blob_copy(blob, twin(across(step)), 0, partner).wait_recv()

    for head in range(heads):
        for source in range(n):
            key_rows[head, pl.ds(source * tok_rows, tok_rows), :] = land_blob[
                source, head, pl.ds(0, tok_rows), :
            ]
            value_rows[head, pl.ds(source * tok_rows, tok_rows), :] = land_blob[
                source, heads + head, pl.ds(0, tok_rows), :
            ]

        def picked(plane, first, count):
            total = land_blob[0, plane, pl.ds(first, count), :].astype(jnp.float32)
            for source in range(1, n):
                total += land_blob[source, plane, pl.ds(first, count), :].astype(jnp.float32)
            return total

        key_rows[head, pl.ds(window, step_count), :] = picked(head, tok_rows, step_count).astype(
            jnp.bfloat16
        )
        value_rows[head, pl.ds(window, step_count), :] = picked(
            heads + head, tok_rows, step_count
        ).astype(jnp.bfloat16)
        half = step_count * group // 2
        for side in range(2):
            step_rows[head, pl.ds(side * half, half), :] = picked(
                2 * head + side, tok_rows + step_count, half
            )
        own_steps = per_shard * group
        own_rows = step_rows[head, pl.ds(me * own_steps, own_steps), :]
        query_rows[head, pl.ds(window_rows, own_steps), :] = own_rows.astype(jnp.bfloat16)
        turn_queries(head, full_tiles, row_tiles)

    for head in range(heads):
        carry(me, head, full_tiles, row_tiles)
        prior_copy(prior.at[head], partner, head, 0, partner).wait_recv()
        carry(partner, head, 0, row_tiles)

    def state_copy(head):
        return pltpu.make_async_copy(state.at[head], state_out.at[head], local_sem.at[2 + head])

    def positions(tile):
        local = tile * TILE + lax.broadcasted_iota(jnp.int32, (TILE, 1), 0)
        return jnp.where(
            local < window_rows,
            local + me * window_rows,
            local - window_rows + window * group + me * (per_shard * group),
        )

    first_offset, lead = place(me)
    for head in range(heads):
        keys_turned = transposed(key_rows[head])
        chunks = padded_keys // LANES
        for chunk in range(chunks):
            piece = keys_turned[:, chunk * LANES : (chunk + 1) * LANES]
            turned[head, chunk, pl.ds(0, LANES), :] = piece
            turned[head, chunk, pl.ds(LANES, LANES), :] = piece

        def state_block(block):
            row = lax.broadcasted_iota(jnp.int32, (LANES, LANES), 0)
            early = row < LANES - lead
            plain = jnp.logical_and(early, first_offset + block == 0)
            factor = jnp.where(plain, 1.0, ROOT_TWO)
            near_row = lax.rem(lead + first_offset + block, LANES)
            far_row = lax.rem(lead + first_offset + block + 1, LANES)
            pieces = []
            for chunk in range(chunks):
                here = turned[head, chunk, pl.ds(lead, LANES), :]
                near = turned[head, chunk, pl.ds(near_row, LANES), :]
                far = turned[head, chunk, pl.ds(far_row, LANES), :]
                both = jnp.where(early, near, far) * factor
                pieces.append((here * both).astype(jnp.bfloat16))
            features = jnp.concatenate(pieces, axis=1)
            return jnp.dot(features, value_rows[head], preferred_element_type=jnp.float32)

        def before(rows):
            return prior[head, rows, :].astype(jnp.float32) if shifted else 0.0

        whole_blocks = state_rows // LANES

        @pl.loop(0, whole_blocks)
        def _(block):
            rows = pl.ds(pl.multiple_of(block * LANES, LANES), LANES)
            state[head, rows, :] = before(rows) + state_block(block)

        rest = state_rows - whole_blocks * LANES
        if rest > 0:
            rows = pl.ds(whole_blocks * LANES, rest)
            state[head, rows, :] = before(rows) + state_block(whole_blocks)[:rest]
        state_copy(head).start()

        @pl.loop(0, row_tiles)
        def _(tile):
            rows = pl.ds(pl.multiple_of(tile * TILE, TILE), TILE)
            scores = lax.dot_general(
                query_rows[head, rows, :],
                key_rows[head],
                contract_last,
                preferred_element_type=jnp.float32,
            )
            position = positions(tile)
            key_index = lax.broadcasted_iota(jnp.int32, scores.shape, 1)
            allowed = position >= key_index * group
            weights = jnp.where(allowed, scores * scores, 0.0).astype(jnp.bfloat16)
            out[head, rows, :] = jnp.dot(
                weights, value_rows[head], preferred_element_type=jnp.float32
            )

    for step in range(1, chips):
        source = across(step)
        for head in range(heads):
            prior_copy(prior.at[head], source, head, 0, partner).wait_recv()
            prior_forward(step, head).start()
            carry(source, head, 0, row_tiles)
            prior_copy(prior.at[head], twin(source), head, 0, partner).wait_recv()
            carry(twin(source), head, 0, row_tiles)

    for head in range(heads):
        for tile in range(row_tiles):
            first = tile * TILE
            token = jnp.floor((positions(tile).astype(jnp.float32) + 0.5) / group)
            place_in_prompt = token + (counts[0] + 1).astype(jnp.float32)
            scale = 1.0 / (LANES * jnp.sqrt(place_in_prompt))
            total = out[head, pl.ds(first, TILE), :] + total_turned[head, tile].T
            total = (total * scale).astype(jnp.bfloat16)
            split = min(max(window_rows - first, 0), TILE)
            if split > 0:
                window_out[head, pl.ds(first, split), :] = total[:split]
            if split < TILE:
                step_out[head, pl.ds(first + split - window_rows, TILE - split), :] = total[split:]
        state_copy(head).wait()

    for slot in range(chips):
        blob_own(slot).wait_send()
        for head in range(heads):
            prior_own(slot, head).wait_send()
    for step in range(1, chips):
        blob_forward(step).wait_send()
        for head in range(heads):
            prior_forward(step, head).wait_send()


def combine(sizes, counts, queries, blob, prior, out_rows):
    n, heads, group, tok_rows, step_count, rows_valid = sizes
    window_rows = tok_rows * group
    lead = max(source * rows_valid % LANES for source in range(n))
    padded_rows = round_up(lead + rows_valid, LANES)
    chunks = out_rows // LANES
    state_rows = round_up(rows_valid, 8)
    padded_keys = round_up(n * tok_rows + step_count, LANES)
    slots = 2 * (n // 2) - 1
    vmem = pl.BlockSpec(memory_space=pltpu.VMEM)
    return pl.pallas_call(
        functools.partial(main_kernel, sizes),
        out_shape=(
            jax.ShapeDtypeStruct((heads, window_rows, LANES), jnp.bfloat16),
            jax.ShapeDtypeStruct((heads, out_rows - window_rows, LANES), jnp.bfloat16),
            jax.ShapeDtypeStruct((heads, state_rows, LANES), jnp.float32),
        ),
        in_specs=[pl.BlockSpec(memory_space=pltpu.SMEM)] + [vmem] * 3,
        out_specs=(vmem, vmem, pl.BlockSpec(memory_space=pl.ANY)),
        scratch_shapes=[
            pltpu.VMEM((heads, out_rows, LANES), jnp.float32),
            pltpu.VMEM((heads, state_rows, LANES), jnp.float32),
            pltpu.VMEM((n,) + blob.shape, jnp.bfloat16),
            pltpu.VMEM((n, heads, padded_rows, LANES), jnp.bfloat16),
            pltpu.VMEM((heads, out_rows, LANES), jnp.bfloat16),
            pltpu.VMEM((heads, chunks, LANES, LANES), jnp.float32),
            pltpu.VMEM((heads, chunks, 2 * LANES, LANES), jnp.float32),
            pltpu.VMEM((LANES, padded_rows), jnp.bfloat16),
            pltpu.VMEM((heads, out_rows // TILE, LANES, TILE), jnp.float32),
            pltpu.VMEM((heads, step_count * group, LANES), jnp.float32),
            pltpu.VMEM((heads, padded_keys, LANES), jnp.bfloat16),
            pltpu.VMEM((heads, padded_keys, LANES), jnp.bfloat16),
            pltpu.VMEM((heads, padded_keys // LANES, 2 * LANES, LANES), jnp.float32),
            pltpu.SemaphoreType.DMA((slots,)),
            pltpu.SemaphoreType.DMA((n,)),
            pltpu.SemaphoreType.DMA((slots, heads)),
            pltpu.SemaphoreType.DMA((n, heads)),
            pltpu.SemaphoreType.DMA((2 + heads,)),
        ],
        compiler_params=pltpu.CompilerParams(
            collective_id=0, has_side_effects=True, vmem_limit_bytes=56 * 2**20
        ),
        name="combine",
    )(counts, queries, blob, prior)


def on_device(queries, keys_values, prior_state, counts, continuation, query_table, pair_table):
    tok_rows, heads, group, head_size = queries.shape
    n = lax.axis_size("ctx")
    shard_index = lax.axis_index("ctx")
    step_count = continuation.shape[0]
    per_shard = step_count // n
    rows_valid = prior_state.shape[1]

    query_pick, pair_pick = pick_rows(
        continuation, query_table.transpose(0, 2, 1, 3), pair_table
    )

    window_planes = keys_values.transpose(2, 1, 0, 3).reshape(2 * heads, tok_rows, head_size)
    step_planes = pair_pick.transpose(2, 1, 0, 3)
    step_planes = step_planes.reshape(2 * heads, step_count, head_size)
    query_planes = query_pick.transpose(2, 0, 1, 3).reshape(
        2 * heads, step_count * group // 2, head_size
    )
    blob = jnp.concatenate([window_planes, step_planes, query_planes], axis=1)
    query_planes = queries.transpose(1, 0, 2, 3).reshape(heads, tok_rows * group, head_size)
    prior = prior_state
    if rows_valid % 16 != 0:
        leads = [source * rows_valid % LANES for source in range(n)]
        prior = lax.dynamic_update_slice(
            jnp.zeros((heads, round_up(max(leads) + rows_valid, LANES), LANES), prior.dtype),
            prior_state,
            (0, shard_index * rows_valid % LANES, 0),
        )
    out_rows = round_up((tok_rows + per_shard) * group, TILE)
    sizes = (n, heads, group, tok_rows, step_count, rows_valid)
    window_out, step_out, state = combine(sizes, counts, query_planes, blob, prior, out_rows)

    decode_state = state
    if rows_valid % 16 != 0:
        decode_state = prior_state.astype(jnp.float32) + state[:, :rows_valid]
    readout = window_out.reshape(heads, tok_rows, group, head_size).transpose(1, 0, 2, 3)
    decode_out = step_out[:, : per_shard * group]
    decode_out = decode_out.reshape(heads, per_shard, group, head_size).transpose(1, 0, 2, 3)
    return (readout, decode_out, decode_state)


def solution(mesh):
    in_specs = (
        P(("groups", "ctx"), "head", None, None),
        P(("groups", "ctx"), "head", None, None),
        P(("groups", "head"), "ctx", None),
        P("groups"),
        P("groups"),
        P("ctx", "head", None, None),
        P("ctx", "head", None, None),
    )
    out_specs = (
        P(("groups", "ctx"), "head", None, None),
        P(("groups", "ctx"), "head", None, None),
        P(("groups", "head"), "ctx", None),
    )
    return jax.shard_map(
        on_device, mesh=mesh, in_specs=in_specs, out_specs=out_specs, check_vma=False
    )
```

profile of v0, /device:TPU:1, one launch (start us, length us, event | category | flops | bytes accessed | tf_op | source)
XLA Modules:
  0.0 55.7 jit_solution(14425136801567141967)
XLA Ops:
  1.3 0.0 copy-start.1
  1.3 0.0 copy-start
  1.3 2.9 %pick_rows.1 = (bf16[32,5,2,128]{3,2,1,0:T(2,128)(2,1)}, bf16[32,2,2,128]{3,2,1,0:T(2,128)(2,1)}) custom-call(s32[32]{0:T(128)} %ids_ref.1, bf16[18992,5,2,128]{3,2,1,0:T(2,128)(2,1)} %bitcast.15, bf16[18992,2,2,128]{3,2,1,0:T(2,128)(2,1)} %pair_table.1), custom_call_target="tpu_custom_call" | custom-call | tf_op jit(solution)/shard_map/pick_rows/pallas_call | solution.py:42
  4.2 0.8 %copy.17 = bf16[2,2,32,128]{3,2,1,0:T(8,128)(2,1)S(1)} copy(bf16[2,2,32,128]{3,0,1,2:T(2,128)(2,1)} %bitcast.22) | data formatting | bytes 65536 | tf_op jit(solution)/shard_map/transpose | solution.py:463
  5.0 0.9 %copy.18 = bf16[2,32,5,128]{3,2,1,0:T(8,128)(2,1)S(1)} copy(bf16[2,32,5,128]{3,0,2,1:T(2,128)(2,1)} %bitcast.21) | data formatting | bytes 163840 | tf_op jit(solution)/shard_map/transpose | solution.py:465
  6.0 0.0 copy-done.1
  6.0 0.7 %pad_maximum_fusion.blob = bf16[4,304,128]{2,1,0:T(8,128)(2,1)} fusion(bf16[4,80,128]{2,1,0:T(8,128)(2,1)S(1)} %reshape.27, bf16[4,32,128]{2,1,0:T(8,128)(2,1)S(1)} %bitcast.20, bf16[4,192,128]{2,1,0:T(8,128)(2,1)S(1)} %bitcast.16), kind=kLoop, calls=%fused_computation | loop fusion | flops 933888 | bytes 622592 | tf_op jit(solution)/shard_map/concatenate | solution.py:468
  6.8 0.0 copy-done
  6.8 0.8 %copy.19.queries = bf16[2,960,128]{2,1,0:T(8,128)(2,1)} copy(bf16[2,960,128]{2,0,1:T(2,128)(2,1)S(1)} %bitcast.17) | data formatting | bytes 983040 | tf_op jit(solution)/shard_map/reshape | solution.py:469
  7.6 41.4 %combine.1 = (bf16[2,960,128]{2,1,0:T(8,128)(2,1)}, bf16[2,64,128]{2,1,0:T(8,128)(2,1)}, f32[2,2064,128]{2,1,0:T(8,128)}) custom-call(s32[1]{0:T(128)S(6)} %copy.23.counts, bf16[2,960,128]{2,1,0:T(8,128)(2,1)} %copy.19.queries, bf16[4,304,128]{2,1,0:T(8,128)(2,1)} %pad_maximum_fusion.blob, bf16[2,2064,128]{2,1,0:T(8,128)(2,1)} %prior.1), custom_call_target="tpu_custom_call" | custom-call | tf_op jit(solution)/shard_map/combine/pallas_call | solution.py:414
  49.0 2.3 %copy.20 = bf16[2,960,128]{2,0,1:T(2,128)(2,1)} copy(bf16[2,960,128]{2,1,0:T(8,128)(2,1)} %get-tuple-element.10) | data formatting | bytes 983040 | tf_op jit(solution)/shard_map/combine/pallas_call | solution.py:414
  51.3 0.7 %slice.3 = bf16[2,40,128]{2,1,0:T(8,128)(2,1)S(1)} slice(bf16[2,64,128]{2,1,0:T(8,128)(2,1)} %get-tuple-element.11), slice={[0:2], [0:40], [0:128]} | slice | bytes 40960 | tf_op jit(solution)/shard_map/slice | solution.py:486
  52.0 0.6 %copy.21 = bf16[2,40,128]{2,0,1:T(2,128)(2,1)} copy(bf16[2,40,128]{2,1,0:T(8,128)(2,1)S(1)} %slice.3) | data formatting | bytes 40960 | tf_op jit(solution)/shard_map/slice | solution.py:486
  52.6 3.1 %copy.24 = f32[2,2064,128]{2,1,0:T(8,128)} copy(f32[2,2064,128]{2,1,0:T(8,128)} %get-tuple-element.18) | data formatting | bytes 4227072
  (2 shorter events, 0.1 us)
Async XLA Ops:
  1.3 4.7 %copy-start.1 = (bf16[192,2,2,128]{3,2,1,0:T(2,128)(2,1)S(1)}, bf16[192,2,2,128]{3,2,1,0:T(2,128)(2,1)}, u32[]{:S(2)}) copy-start(bf16[192,2,2,128]{3,2,1,0:T(2,128)(2,1)} %param.8) | copy-start | bytes 589828
  1.3 5.5 %copy-start = (bf16[192,2,5,128]{3,1,2,0:T(2,128)(2,1)S(1)}, bf16[192,2,5,128]{3,1,2,0:T(2,128)(2,1)}, u32[]{:S(2)}) copy-start(bf16[192,2,5,128]{3,1,2,0:T(2,128)(2,1)} %param.7) | copy-start | bytes 1474564
where the time goes:
time: 56.2 us; the launch traced here: 55.7 us
  Pallas kernels  44.3 us (79%)
  local copies, waits for them, and re-layouts  9.32 us (17%)
  between operations  1.34 us (2%)
  other arithmetic  0.74 us (1%)
    pallas_call x1, Pallas kernels, combine(): pl.pallas_call(functools.partial(main_kernel, sizes), out_shape=(jax.Shap...  41.4 us
    unnamed x5, local copies, waits for them, and re-layouts  3.06 us
    pallas_call x1, Pallas kernels, pick_rows(): pl.pallas_call(pick_kernel, out_shape=(jax.ShapeDtypeStruct((steps,) + qu...  2.93 us
    pallas_call x1, local copies, waits for them, and re-layouts, combine(): pl.pallas_call(functools.partial(main_kernel, sizes), out_shape=(jax.Shap...  2.31 us
    slice x2, local copies, waits for them, and re-layouts, on_device(): decode_out = step_out[:, :per_shard * group]  1.35 us

commit v1 on v0

--- a/solution.py
+++ b/solution.py
@@ -7,10 +7,12 @@
 from jax.experimental.pallas import tpu as pltpu
 from jax.sharding import PartitionSpec as P
 
+
 ROOT_TWO = 2.0**0.5
 MESH = pl.DeviceIdType.MESH
 TILE = 256
 LANES = 128
+CONTRACT_LAST = (((1,), (1,)), ((), ()))
 
 
 def round_up(number, multiple):
@@ -447,7 +449,7 @@
     )(counts, queries, blob, prior)
 
 
-def on_device(queries, keys_values, prior_state, counts, continuation, query_table, pair_table):
+def on_device_gather(queries, keys_values, prior_state, counts, continuation, query_table, pair_table):
     tok_rows, heads, group, head_size = queries.shape
     n = lax.axis_size("ctx")
     shard_index = lax.axis_index("ctx")
@@ -488,6 +490,381 @@
     return (readout, decode_out, decode_state)
 
 
+def identity():
+    row = lax.broadcasted_iota(jnp.int32, (LANES, LANES), 0)
+    column = lax.broadcasted_iota(jnp.int32, (LANES, LANES), 1)
+    return (row == column).astype(jnp.bfloat16)
+
+
+def turned_rows(rows):
+    return lax.dot_general(
+        identity(), rows, CONTRACT_LAST, preferred_element_type=jnp.float32
+    )
+
+
+def turn_queries(load, count, plain, scaled):
+    for chunk in range(count // LANES):
+        piece = turned_rows(load(chunk * LANES))
+        twice = piece * ROOT_TWO
+        plain[chunk] = piece
+        scaled[chunk, pl.ds(0, LANES), :] = twice
+        scaled[chunk, pl.ds(LANES, LANES), :] = twice
+
+
+def carry_tile(state_turned, first_offset, plain, scaled, tile):
+    blocks = state_turned.shape[1] // LANES
+    columns = []
+    for side in range(TILE // LANES):
+        chunk = tile * (TILE // LANES) + side
+        here = plain[chunk]
+        pieces = []
+        for block in range(blocks):
+            other = scaled[chunk, pl.ds(first_offset + block, LANES), :]
+            if block == 0:
+                other = jnp.where(first_offset == 0, here, other)
+            pieces.append((here * other).astype(jnp.bfloat16))
+        columns.append(jnp.concatenate(pieces, axis=0))
+    features = jnp.concatenate(columns, axis=1)
+    return jnp.dot(state_turned[...], features, preferred_element_type=jnp.float32).T
+
+
+def chip_place(rows_valid):
+    first = lax.div(lax.axis_index("ctx"), 2) * (2 * rows_valid)
+    return lax.div(first, LANES), pl.multiple_of(lax.rem(first, LANES), 16)
+
+
+def early_kernel(rows_valid, queries, own, other, turned, local, rows, plain, scaled):
+    heads, padded = turned.shape[0], turned.shape[2]
+    first_offset, lead = chip_place(rows_valid)
+    core = lax.rem(lax.axis_index("ctx"), 2)
+    count = local.shape[1]
+    for head in range(heads):
+        rows[pl.ds(0, LANES), :] = jnp.zeros((LANES, LANES), rows.dtype)
+        spare = padded - 2 * rows_valid
+        rows[pl.ds(padded - spare, spare), :] = jnp.zeros((spare, LANES), rows.dtype)
+        for source, index in ((own, core), (other, 1 - core)):
+            start = pl.multiple_of(lead + index * rows_valid, 16)
+            rows[pl.ds(start, rows_valid), :] = source[head]
+        for first in range(0, padded, 2 * LANES):
+            size = min(2 * LANES, padded - first)
+            turned[head, :, pl.ds(first, size)] = turned_rows(
+                rows[pl.ds(first, size), :]
+            ).astype(turned.dtype)
+        turn_queries(
+            lambda at: queries[head, pl.ds(at, LANES), :], count, plain, scaled
+        )
+        for tile in range(count // TILE):
+            local[head, pl.ds(tile * TILE, TILE), :] = carry_tile(
+                turned.at[head], first_offset, plain, scaled, tile
+            )
+
+
+def remote_kernel(rows_valid, queries, turned, partial, plain, scaled):
+    first_offset, _ = chip_place(rows_valid)
+    count = partial.shape[1]
+    for head in range(turned.shape[0]):
+        turn_queries(
+            lambda at: queries[head, pl.ds(at, LANES), :], count, plain, scaled
+        )
+        for tile in range(count // TILE):
+            partial[head, pl.ds(tile * TILE, TILE), :] = carry_tile(
+                turned.at[head], first_offset, plain, scaled, tile
+            ).astype(partial.dtype)
+
+
+def fill_tail(head, queries, steps, first, tail):
+    window = queries.shape[1] - first
+    count = steps.shape[1]
+    tail[...] = jnp.zeros_like(tail)
+    tail[pl.ds(0, window), :] = queries[head, pl.ds(first, window), :]
+    tail[pl.ds(window, count), :] = steps[head]
+
+
+def remote_tail_kernel(rows_valid, first, queries, steps, turned, partial, tail, plain, scaled):
+    first_offset, _ = chip_place(rows_valid)
+    for head in range(turned.shape[0]):
+        fill_tail(head, queries, steps, first, tail)
+        turn_queries(lambda at: tail[pl.ds(at, LANES), :], TILE, plain, scaled)
+        rows = carry_tile(turned.at[head], first_offset, plain, scaled, 0)
+        partial[head] = rows[: partial.shape[1]].astype(partial.dtype)
+
+
+def late_kernel(
+    sizes,
+    queries,
+    steps,
+    turned,
+    local,
+    own_pairs,
+    twin_pairs,
+    across_pairs,
+    far_pairs,
+    step_pairs,
+    prior,
+    result,
+    state_out,
+    tail,
+    plain,
+    scaled,
+    key_rows,
+    value_rows,
+    keys_plain,
+    keys_scaled,
+    delta,
+    state,
+    state_sem,
+):
+    n, heads, group, tok_rows, step_count, rows_valid = sizes
+    first_offset, _ = chip_place(rows_valid)
+    me = lax.axis_index("ctx")
+    twin = me + 1 - 2 * lax.rem(me, 2)
+    window = n * tok_rows
+    window_rows = tok_rows * group
+    per_shard = step_count // n
+    first_tail = local.shape[1]
+    padded_keys = key_rows.shape[1]
+    chunks = padded_keys // LANES
+    blocks = delta.shape[0] // LANES
+    my_first = me * rows_valid
+    my_offset = lax.div(my_first, LANES)
+    my_lead = pl.multiple_of(lax.rem(my_first, LANES), 8)
+    places = (
+        (own_pairs, me),
+        (twin_pairs, twin),
+        (across_pairs, lax.rem(me + 2, n)),
+        (far_pairs, lax.rem(twin + 2, n)),
+    )
+
+    def state_copy(head):
+        return pltpu.make_async_copy(state.at[head], state_out.at[head], state_sem.at[head])
+
+    for head in range(heads):
+        for plane, target in ((0, key_rows), (1, value_rows)):
+            for pairs, source in places:
+                start = pl.multiple_of(source * tok_rows, 16)
+                target[head, pl.ds(start, tok_rows), :] = pairs[plane, head]
+            target[head, pl.ds(window, step_count), :] = step_pairs[plane, head]
+            spare = padded_keys - window - step_count
+            if spare > 0:
+                target[head, pl.ds(window + step_count, spare), :] = jnp.zeros(
+                    (spare, LANES), target.dtype
+                )
+        for chunk in range(chunks):
+            piece = turned_rows(key_rows[head, pl.ds(chunk * LANES, LANES), :])
+            twice = piece * ROOT_TWO
+            keys_plain[chunk] = piece
+            keys_scaled[chunk, pl.ds(0, LANES), :] = twice
+            keys_scaled[chunk, pl.ds(LANES, LANES), :] = twice
+
+        def key_features(block, maybe_plain):
+            pieces = []
+            for chunk in range(chunks):
+                here = keys_plain[chunk]
+                other = keys_scaled[chunk, pl.ds(my_offset + block, LANES), :]
+                if maybe_plain:
+                    other = jnp.where(my_offset == 0, here, other)
+                pieces.append((here * other).astype(jnp.bfloat16))
+            return jnp.concatenate(pieces, axis=1)
+
+        def add_block(features, first):
+            delta[pl.ds(first, features.shape[0]), :] = jnp.dot(
+                features, value_rows[head], preferred_element_type=jnp.float32
+            )
+
+        odd = 1 if blocks % 2 else 2
+        for block in range(odd):
+            add_block(key_features(block, block == 0), block * LANES)
+
+        @pl.loop(0, (blocks - odd) // 2)
+        def _(pair):
+            block = odd + 2 * pair
+            both = jnp.concatenate(
+                [key_features(block, False), key_features(block + 1, False)], axis=0
+            )
+            add_block(both, pl.multiple_of(block * LANES, LANES))
+
+        state[head] = prior[head].astype(jnp.float32) + delta[pl.ds(my_lead, rows_valid), :]
+        state_copy(head).start()
+
+    for head in range(heads):
+        fill_tail(head, queries, steps, first_tail, tail)
+        turn_queries(lambda at: tail[pl.ds(at, LANES), :], TILE, plain, scaled)
+        carried_tail = carry_tile(turned.at[head], first_offset, plain, scaled, 0)
+        for first in range(0, result.shape[1], TILE):
+            last = first >= first_tail
+            rows = tail[...] if last else queries[head, pl.ds(first, TILE), :]
+            scores = lax.dot_general(
+                rows, key_rows[head], CONTRACT_LAST, preferred_element_type=jnp.float32
+            )
+            at = first + lax.broadcasted_iota(jnp.int32, (TILE, 1), 0)
+            position = jnp.where(
+                at < window_rows,
+                at + me * window_rows,
+                at - window_rows + window * group + me * (per_shard * group),
+            )
+            key_index = lax.broadcasted_iota(jnp.int32, scores.shape, 1)
+            weights = jnp.where(position >= key_index * group, scores * scores, 0.0)
+            total = jnp.dot(
+                weights.astype(jnp.bfloat16), value_rows[head], preferred_element_type=jnp.float32
+            )
+            carried = carried_tail if last else local[head, pl.ds(first, TILE), :]
+            size = min(TILE, result.shape[1] - first)
+            result[head, pl.ds(first, size), :] = (total + carried)[:size]
+    for head in range(heads):
+        state_copy(head).wait()
+
+
+def vmem_call(kernel, out_shape, operands, scratch, limit, out_specs=None):
+    vmem = pl.BlockSpec(memory_space=pltpu.VMEM)
+    return pl.pallas_call(
+        kernel,
+        out_shape=out_shape,
+        in_specs=[vmem] * len(operands),
+        out_specs=out_specs if out_specs is not None else jax.tree.map(lambda _: vmem, out_shape),
+        scratch_shapes=scratch,
+        compiler_params=pltpu.CompilerParams(vmem_limit_bytes=limit * 2**20),
+    )(*operands)
+
+
+def turn_scratch(columns):
+    chunks = columns // LANES
+    return [
+        pltpu.VMEM((chunks, LANES, LANES), jnp.float32),
+        pltpu.VMEM((chunks, 2 * LANES, LANES), jnp.float32),
+    ]
+
+
+def on_device_exchange(
+    queries, keys_values, prior, counts, continuation, query_table, pair_table
+):
+    tok_rows, heads, group, head_size = queries.shape
+    n = lax.axis_size("ctx")
+    me = lax.axis_index("ctx")
+    core, chip = lax.rem(me, 2), lax.div(me, 2)
+    step_count = continuation.shape[0]
+    per_shard = step_count // n
+    step_rows = per_shard * group
+    rows_valid = prior.shape[1]
+    window_rows = tok_rows * group
+    early = window_rows // TILE * TILE
+    rows_chip = 2 * rows_valid
+    padded = max(
+        round_up(chip_at * rows_chip % LANES + rows_chip, LANES) for chip_at in range(n // 2)
+    )
+    blocks = max(
+        round_up(source * rows_valid % LANES + rows_valid, LANES) // LANES for source in range(n)
+    )
+    padded_keys = round_up(n * tok_rows + step_count, LANES)
+    bf16, f32 = jnp.bfloat16, jnp.float32
+    shape = jax.ShapeDtypeStruct
+
+    def swap_across(value):
+        return lax.ppermute(value, "ctx", [(i, (i + 2) % n) for i in range(n)])
+
+    def swap_twin(value):
+        return lax.ppermute(value, "ctx", [(i, i ^ 1) for i in range(n)])
+
+    def query_planes(value):
+        return value.transpose(1, 0, 2, 3).reshape(heads, -1, head_size)
+
+    def pair_planes(value):
+        return value.transpose(2, 1, 0, 3)
+
+    across_queries = swap_across(queries)
+    across_pairs = swap_across(keys_values)
+    twin_prior = swap_twin(prior)
+    twin_pairs = swap_twin(keys_values)
+    query_pick, pair_pick = pick_rows(
+        continuation, query_table.transpose(0, 2, 1, 3), pair_table
+    )
+    query_chip = query_pick + swap_twin(query_pick)
+    pair_chip = pair_pick + swap_twin(pair_pick)
+    mine = [
+        lax.dynamic_slice_in_dim(query_chip, (core + 2 * at) * per_shard, per_shard)
+        for at in range(n // 2)
+    ]
+    send = jnp.concatenate(
+        [part.reshape(step_rows, heads, head_size) for part in mine]
+        + [pair_chip.reshape(step_count * heads, 2, head_size)]
+    )
+    steps = send + swap_across(send)
+    step_pairs = pair_planes(steps[n // 2 * step_rows :].reshape(step_count, heads, 2, head_size))
+    step_queries = steps[: n // 2 * step_rows].transpose(1, 0, 2)
+    own_steps = lax.dynamic_slice_in_dim(step_queries, chip * step_rows, step_rows, 1)
+    across_steps = lax.dynamic_slice_in_dim(step_queries, (1 - chip) * step_rows, step_rows, 1)
+
+    own_rows = query_planes(queries)
+    turned, local = vmem_call(
+        functools.partial(early_kernel, rows_valid),
+        (shape((heads, LANES, padded), bf16), shape((heads, early, LANES), f32)),
+        (own_rows, prior, twin_prior),
+        [pltpu.VMEM((padded, LANES), bf16)] + turn_scratch(early),
+        16,
+    )
+    across_rows = query_planes(across_queries)
+    partial = vmem_call(
+        functools.partial(remote_kernel, rows_valid),
+        shape((heads, early, LANES), bf16),
+        (across_rows, turned),
+        turn_scratch(early),
+        16,
+    )
+    got = swap_across(partial)
+    partial_tail = vmem_call(
+        functools.partial(remote_tail_kernel, rows_valid, early),
+        shape((heads, window_rows - early + step_rows, LANES), bf16),
+        (across_rows, across_steps, turned),
+        [pltpu.VMEM((TILE, LANES), bf16)] + turn_scratch(TILE),
+        16,
+    )
+    got_tail = swap_across(partial_tail)
+    far_pairs = swap_twin(across_pairs)
+    sizes = (n, heads, group, tok_rows, step_count, rows_valid)
+    vmem = pl.BlockSpec(memory_space=pltpu.VMEM)
+    chunks = padded_keys // LANES
+    result, decode_state = vmem_call(
+        functools.partial(late_kernel, sizes),
+        (
+            shape((heads, window_rows + step_rows, LANES), f32),
+            shape((heads, rows_valid, LANES), f32),
+        ),
+        (
+            own_rows,
+            own_steps,
+            turned,
+            local,
+            pair_planes(keys_values),
+            pair_planes(twin_pairs),
+            pair_planes(across_pairs),
+            pair_planes(far_pairs),
+            step_pairs,
+            prior,
+        ),
+        [pltpu.VMEM((TILE, LANES), bf16)]
+        + turn_scratch(TILE)
+        + [
+            pltpu.VMEM((heads, padded_keys, LANES), bf16),
+            pltpu.VMEM((heads, padded_keys, LANES), bf16),
+            pltpu.VMEM((chunks, LANES, LANES), f32),
+            pltpu.VMEM((chunks, 2 * LANES, LANES), f32),
+            pltpu.VMEM((blocks * LANES, LANES), f32),
+            pltpu.VMEM((heads, rows_valid, LANES), f32),
+            pltpu.SemaphoreType.DMA((heads,)),
+        ],
+        24,
+        (vmem, pl.BlockSpec(memory_space=pl.ANY)),
+    )
+    window_at = counts[0] + 1 + me * tok_rows + jnp.arange(window_rows, dtype=jnp.int32) // group
+    steps_at = counts[0] + 1 + n * tok_rows + me * per_shard
+    steps_at = steps_at + jnp.arange(step_rows, dtype=jnp.int32) // group
+    scale = 1.0 / (head_size * jnp.sqrt(jnp.concatenate([window_at, steps_at]).astype(f32)))
+    total = result + jnp.concatenate([got, got_tail], axis=1).astype(f32)
+    total = (total * scale[None, :, None]).astype(bf16)
+    readout = total[:, :window_rows].reshape(heads, tok_rows, group, head_size)
+    decode_out = total[:, window_rows:].reshape(heads, per_shard, group, head_size)
+    return (readout.transpose(1, 0, 2, 3), decode_out.transpose(1, 0, 2, 3), decode_state)
+
+
 def solution(mesh):
     in_specs = (
         P(("groups", "ctx"), "head", None, None),
@@ -503,6 +880,13 @@
         P(("groups", "ctx"), "head", None, None),
         P(("groups", "head"), "ctx", None),
     )
+
+    def on_device(*arguments):
+        n, rows_valid = lax.axis_size("ctx"), arguments[2].shape[1]
+        if n == 4 and rows_valid % 16 == 0:
+            return on_device_exchange(*arguments)
+        return on_device_gather(*arguments)
+
     return jax.shard_map(
         on_device, mesh=mesh, in_specs=in_specs, out_specs=out_specs, check_vma=False
     )

time: 56.2 us -> 43.6 us (0.78)
  Pallas kernels: 44.3 us -> 24.2 us
  starting transfers between devices: 0 us -> 8.47 us
  local copies, waits for them, and re-layouts: 9.32 us -> 3.25 us
  waiting for transfers between devices: 0 us -> 3.66 us
  other arithmetic: 0.74 us -> 2.18 us
    pallas_call x1 -> x4, Pallas kernels: 41.4 us -> 21.3 us  [vmem_call(): pl.pallas_call(kernel, out_shape=out_shape, in_specs=[vmem] * len(operand...]
    ppermute x0 -> x10, starting transfers between devices: none -> 8.47 us  [the longest x5 5.74 us: swap_across(): return lax.ppermute(value, 'ctx', [(i, (i + 2) % n) for i in range(n)])]
    ppermute x0 -> x10, waiting for transfers between devices: none -> 3.66 us  [the longest x5 3.2 us: swap_across(): return lax.ppermute(value, 'ctx', [(i, (i + 2) % n) for i in range(n)])]
    unnamed x5 -> x7, local copies, waits for them, and re-layouts: 3.06 us -> 0.04 us
    pallas_call x1 -> x0, local copies, waits for them, and re-layouts: 2.31 us -> none  [combine(): pl.pallas_call(functools.partial(main_kernel, sizes), out_shape=(jax.Shap...]
    add x0 -> x5, other arithmetic: none -> 1.86 us  [the longest x1 1.02 us: on_device_exchange(): query_chip = query_pick + swap_twin(query_pick)]
    transpose x3 -> x0, local copies, waits for them, and re-layouts: 1.7 us -> none  [the longest x1 0.91 us: on_device(): query_pick.transpose(2, 0, 1, 3)]
    concatenate x1, other arithmetic: 0.74 us -> 0.01 us  [on_device_exchange(): jnp.concatenate([part.reshape(step_rows, heads, head_size) for part in mi...]
  transfers between devices with their start and end apart: 0 -> 10, of which waited for: 0 -> 2; matrix products, arithmetic and copies ran while one was open for 0% -> 7% of each run, Pallas kernels for 0% -> 56%
where the time goes in v1:
time: 43.6 us; the launch traced here: 43.3 us
  Pallas kernels  24.2 us (56%)
  starting transfers between devices  8.47 us (19%)
  waiting for transfers between devices  3.66 us (8%)
  local copies, waits for them, and re-layouts  3.25 us (7%)
  other arithmetic  2.18 us (5%)
  between operations  1.55 us (4%)
    pallas_call x4, Pallas kernels, vmem_call(): pl.pallas_call(kernel, out_shape=out_shape, in_specs=[vmem] * len(operand...  21.3 us
    ppermute x5, starting transfers between devices, swap_across(): return lax.ppermute(value, 'ctx', [(i, (i + 2) % n) for i in range(n)])  5.74 us
    ppermute x5, waiting for transfers between devices, swap_across(): return lax.ppermute(value, 'ctx', [(i, (i + 2) % n) for i in range(n)])  3.2 us
    pallas_call x1, Pallas kernels, pick_rows(): pl.pallas_call(pick_kernel, out_shape=(jax.ShapeDtypeStruct((steps,) + qu...  2.87 us
    ppermute x5, starting transfers between devices, swap_twin(): return lax.ppermute(value, 'ctx', [(i, i ^ 1) for i in range(n)])  2.73 us
    slice x2, local copies, waits for them, and re-layouts, on_device_exchange(): readout = total[:, :window_rows].reshape(heads, tok_rows, group, head_size)  1.32 us
    reshape x2, local copies, waits for them, and re-layouts, query_planes(): return value.transpose(1, 0, 2, 3).reshape(heads, -1, head_size)  1.16 us
    add x1, other arithmetic, on_device_exchange(): query_chip = query_pick + swap_twin(query_pick)  1.02 us
  transfers between devices with their start and end apart: 10, of which 2 were waited for; matrix products, arithmetic and copies ran while one was open for 7% of the time, Pallas kernels for 56%

profile of v1, /device:TPU:1, one launch (start us, length us, event | category | flops | bytes accessed | tf_op | source)
XLA Modules:
  0.0 43.3 jit_solution(8129929993458619446)
XLA Ops:
  0.6 0.1 collective-permute-start.3
  0.7 2.7 %collective-permute-start.7 = (bf16[192,2,5,128]{3,1,2,0:T(2,128)(2,1)}, bf16[192,2,5,128]{3,1,2,0:T(2,128)(2,1)}, u32[]{:S(2)}, u32[]{:S(2)}) collective-permute-start(bf16[192,2,5,128]{3,1,2,0:T(2,128)(2,1)} %param.7), channel_id=1, source_target_pairs={{0,8},{4,12},{8,0},{12,4},{1,9},{5,13},{9,1},{13,5},{2,10},{6,14},... | collective-permute-start | bytes 1474568 | tf_op jit(solution)/shard_map/ppermute | solution.py:762
  3.4 0.0 copy-start.2
  3.4 0.0 copy-start.1
  3.4 2.9 %pick_rows.1 = (bf16[32,5,2,128]{3,2,1,0:T(2,128)(2,1)}, bf16[32,2,2,128]{3,2,1,0:T(2,128)(2,1)}) custom-call(s32[32]{0:T(128)} %ids_ref.1, bf16[18992,5,2,128]{3,2,1,0:T(2,128)(2,1)} %bitcast.36, bf16[18992,2,2,128]{3,2,1,0:T(2,128)(2,1)} %pair_table.1), custom_call_target="tpu_custom_call" | custom-call | tf_op jit(solution)/shard_map/pick_rows/pallas_call | solution.py:44
  6.3 0.0 copy-start
  6.3 0.5 %collective-permute-start = (bf16[32,5,2,128]{3,2,1,0:T(2,128)(2,1)}, bf16[32,5,2,128]{3,2,1,0:T(2,128)(2,1)}, u32[]{:S(2)}, u32[]{:S(2)}) collective-permute-start(bf16[32,5,2,128]{3,2,1,0:T(2,128)(2,1)} %get-tuple-element.9), channel_id=1, source_target_pairs={{0,4},{4,0},{8,12},{12,8},{1,5},{5,1},{9,13},{13,9},{2,6},{6,2},{1... | collective-permute-start | bytes 245768 | tf_op jit(solution)/shard_map/ppermute | solution.py:765
  6.8 0.1 collective-permute-start.1
  6.9 0.0 copy-done.2
  7.0 0.1 collective-permute-start.5
  7.1 0.0 copy-done.1
  7.1 0.1 copy.29.queries
  7.8 0.4 %collective-permute-done.1 = bf16[32,2,2,128]{3,2,1,0:T(2,128)(2,1)S(1)} collective-permute-done((bf16[32,2,2,128]{3,2,1,0:T(2,128)(2,1)}, bf16[32,2,2,128]{3,2,1,0:T(2,128)(2,1)S(1)}, u32[]{:S(2)}, u32[]{:S(2)}) %collective-permute-start.1) | collective-permute-done | bytes 32800 | tf_op jit(solution)/shard_map/ppermute | solution.py:765
  8.3 0.2 collective-permute-start.4
  8.5 0.8 %add.74 = bf16[32,2,2,128]{3,2,1,0:T(2,128)(2,1)S(1)} add(bf16[32,2,2,128]{3,2,1,0:T(2,128)(2,1)} %get-tuple-element.10, bf16[32,2,2,128]{3,2,1,0:T(2,128)(2,1)S(1)} %collective-permute-done.1) | non-fusion elementwise | flops 16384 | bytes 98304 | tf_op jit(solution)/shard_map/add | solution.py:781
  9.3 0.0 collective-permute-done
  9.3 1.0 %add.70 = bf16[32,5,2,128]{3,2,1,0:T(2,128)(2,1)S(1)} add(bf16[32,5,2,128]{3,2,1,0:T(2,128)(2,1)} %get-tuple-element.9, bf16[32,5,2,128]{3,2,1,0:T(2,128)(2,1)} %collective-permute-done) | non-fusion elementwise | flops 40960 | bytes 245760 | tf_op jit(solution)/shard_map/add | solution.py:780
  10.4 1.6 %collective-permute-start.2 = (bf16[144,2,128]{2,0,1:T(8,128)(2,1)S(1)}, bf16[144,2,128]{2,0,1:T(8,128)(2,1)S(1)}, u32[]{:S(2)}, u32[]{:S(2)}) collective-permute-start(bf16[144,2,128]{2,0,1:T(8,128)(2,1)S(1)} %pad_maximum_fusion), channel_id=1, source_target_pairs={{0,8},{4,12},{8,0},{12,4},{1,9},{5,13},{9,1},{13,5},{2,10},{6,14},... | collective-permute-start | bytes 221192 | tf_op jit(solution)/shard_map/ppermute | solution.py:762
  12.0 3.2 %collective-permute-done.7 = bf16[192,2,5,128]{3,1,2,0:T(2,128)(2,1)} collective-permute-done((bf16[192,2,5,128]{3,1,2,0:T(2,128)(2,1)}, bf16[192,2,5,128]{3,1,2,0:T(2,128)(2,1)}, u32[]{:S(2)}, u32[]{:S(2)}) %collective-permute-start.7) | collective-permute-done | bytes 491552 | tf_op jit(solution)/shard_map/ppermute | solution.py:762
  15.2 1.1 %copy.30.queries = bf16[2,960,128]{2,1,0:T(8,128)(2,1)S(1)} copy(bf16[2,960,128]{2,0,1:T(2,128)(2,1)} %bitcast.14) | data formatting | bytes 983040 | tf_op jit(solution)/shard_map/reshape | solution.py:768
  16.3 0.0 collective-permute-done.3.other
  16.3 0.0 copy-done
  16.3 5.1 %shard_map.94 = (bf16[2,128,4224]{2,1,0:T(8,128)(2,1)S(1)}, f32[2,768,128]{2,1,0:T(8,128)S(1)}) custom-call(bf16[2,960,128]{2,1,0:T(8,128)(2,1)S(1)} %copy.29.queries, bf16[2,2064,128]{2,1,0:T(8,128)(2,1)S(1)} %copy-done, bf16[2,2064,128]{2,1,0:T(8,128)(2,1)S(1)} %collective-permute-done.3.other), custom_call_target="tpu_custom_call" | custom-call | tf_op jit(solution)/shard_map/pallas_call | solution.py:719
  21.4 4.0 %shard_map.96 = bf16[2,768,128]{2,1,0:T(8,128)(2,1)S(1)} custom-call(bf16[2,960,128]{2,1,0:T(8,128)(2,1)S(1)} %copy.30.queries, bf16[2,128,4224]{2,1,0:T(8,128)(2,1)S(1)} %get-tuple-element.11.turned), custom_call_target="tpu_custom_call" | custom-call | tf_op jit(solution)/shard_map/pallas_call | solution.py:719
  25.5 1.2 %collective-permute-start.8 = (bf16[2,768,128]{2,1,0:T(8,128)(2,1)S(1)}, bf16[2,768,128]{2,1,0:T(8,128)(2,1)S(1)}, u32[]{:S(2)}, u32[]{:S(2)}) collective-permute-start(bf16[2,768,128]{2,1,0:T(8,128)(2,1)S(1)} %shard_map.96), channel_id=1, source_target_pairs={{0,8},{4,12},{8,0},{12,4},{1,9},{5,13},{9,1},{13,5},{2,10},{6,14},... | collective-permute-start | bytes 1179656 | tf_op jit(solution)/shard_map/ppermute | solution.py:762
  26.7 0.0 collective-permute-done.2
  26.8 0.0 collective-permute-done.5
  26.8 1.8 %collective-permute-start.6 = (bf16[192,2,2,128]{3,0,1,2:T(8,128)(2,1)S(1)}, bf16[192,2,2,128]{3,0,1,2:T(8,128)(2,1)S(1)}, u32[]{:S(2)}, u32[]{:S(2)}) collective-permute-start(bf16[192,2,2,128]{3,0,1,2:T(8,128)(2,1)S(1)} %collective-permute-done.5), channel_id=1, source_target_pairs={{0,4},{4,0},{8,12},{12,8},{1,5},{5,1},{9,13},{13,9},{2,6},{6,2},{1... | collective-permute-start | bytes 589832 | tf_op jit(solution)/shard_map/ppermute | solution.py:765
  28.6 1.7 %shard_map.97 = bf16[2,232,128]{2,1,0:T(8,128)(2,1)S(1)} custom-call(bf16[2,960,128]{2,1,0:T(8,128)(2,1)S(1)} %copy.30.queries, bf16[2,40,128]{2,1,0:T(8,128)(2,1)S(1)} %get-tuple-element.19.steps, bf16[2,128,4224]{2,1,0:T(8,128)(2,1)S(1)} %get-tuple-element.11.turned), custom_call_target="tpu_custom_call" | custom-call | tf_op jit(solution)/shard_map/pallas_call | solution.py:719
  30.3 0.1 collective-permute-start.9
  30.4 0.1 fusion.5
  30.5 0.0 collective-permute-done.4
  30.5 0.0 collective-permute-done.6
  30.5 10.5 %shard_map.95 = (f32[2,1000,128]{2,1,0:T(8,128)S(1)}, f32[2,2064,128]{2,1,0:T(8,128)}) custom-call(bf16[2,960,128]{2,1,0:T(8,128)(2,1)S(1)} %copy.29.queries, bf16[2,40,128]{2,1,0:T(8,128)(2,1)S(1)} %get-tuple-element.20.steps, bf16[2,128,4224]{2,1,0:T(8,128)(2,1)S(1)} %get-tuple-element.11.turned, f32[2,768,128]{2,1,0:T(8,128)S(1)} %get-tuple-element.12.local, ...), custom_call_target="tpu_custom_call" | custom-call | tf_op jit(solution)/shard_map/pallas_call | solution.py:719
  41.0 0.0 collective-permute-done.9
  41.1 0.0 collective-permute-done.8
  41.1 0.2 multiply_convert_fusion
  41.4 1.3 %copy.32 = bf16[2,960,128]{2,0,1:T(2,128)(2,1)} copy(bf16[2,960,128]{2,1,0:T(8,128)(2,1)S(1)} %slice.18) | data formatting | bytes 983040 | tf_op jit(solution)/shard_map/slice | solution.py:863
  42.6 0.6 %copy.33 = bf16[2,40,128]{2,0,1:T(2,128)(2,1)} copy(bf16[2,40,128]{2,1,0:T(8,128)(2,1)S(1)} %slice.19) | data formatting | bytes 40960 | tf_op jit(solution)/shard_map/slice | solution.py:864
  (15 shorter events, 0.2 us)
Async XLA Ops:
  0.6 15.7 %collective-permute-start.3 = (bf16[2,2064,128]{2,1,0:T(8,128)(2,1)}, bf16[2,2064,128]{2,1,0:T(8,128)(2,1)S(1)}, u32[]{:S(2)}, u32[]{:S(2)}) collective-permute-start(bf16[2,2064,128]{2,1,0:T(8,128)(2,1)} %prior.1), channel_id=1, source_target_pairs={{0,4},{4,0},{8,12},{12,8},{1,5},{5,1},{9,13},{13,9},{2,6},{6,2},{1... | collective-permute-start | bytes 3170312 | tf_op jit(solution)/shard_map/ppermute | solution.py:765
  0.7 14.5 %collective-permute-start.7 = (bf16[192,2,5,128]{3,1,2,0:T(2,128)(2,1)}, bf16[192,2,5,128]{3,1,2,0:T(2,128)(2,1)}, u32[]{:S(2)}, u32[]{:S(2)}) collective-permute-start(bf16[192,2,5,128]{3,1,2,0:T(2,128)(2,1)} %param.7), channel_id=1, source_target_pairs={{0,8},{4,12},{8,0},{12,4},{1,9},{5,13},{9,1},{13,5},{2,10},{6,14},... | collective-permute-start | bytes 1474568 | tf_op jit(solution)/shard_map/ppermute | solution.py:762
  3.4 3.5 %copy-start.2 = (bf16[192,2,2,128]{3,2,1,0:T(2,128)(2,1)S(1)}, bf16[192,2,2,128]{3,2,1,0:T(2,128)(2,1)}, u32[]{:S(2)}) copy-start(bf16[192,2,2,128]{3,2,1,0:T(2,128)(2,1)} %param.8) | copy-start | bytes 589828
  3.4 3.7 %copy-start.1 = (bf16[192,2,5,128]{3,1,2,0:T(2,128)(2,1)S(1)}, bf16[192,2,5,128]{3,1,2,0:T(2,128)(2,1)}, u32[]{:S(2)}) copy-start(bf16[192,2,5,128]{3,1,2,0:T(2,128)(2,1)} %param.7) | copy-start | bytes 1474564
  6.3 10.1 %copy-start = (bf16[2,2064,128]{2,1,0:T(8,128)(2,1)S(1)}, bf16[2,2064,128]{2,1,0:T(8,128)(2,1)}, u32[]{:S(2)}) copy-start(bf16[2,2064,128]{2,1,0:T(8,128)(2,1)} %prior.1) | copy-start | bytes 3170308
  6.3 3.0 %collective-permute-start = (bf16[32,5,2,128]{3,2,1,0:T(2,128)(2,1)}, bf16[32,5,2,128]{3,2,1,0:T(2,128)(2,1)}, u32[]{:S(2)}, u32[]{:S(2)}) collective-permute-start(bf16[32,5,2,128]{3,2,1,0:T(2,128)(2,1)} %get-tuple-element.9), channel_id=1, source_target_pairs={{0,4},{4,0},{8,12},{12,8},{1,5},{5,1},{9,13},{13,9},{2,6},{6,2},{1... | collective-permute-start | bytes 245768 | tf_op jit(solution)/shard_map/ppermute | solution.py:765
  6.8 1.4 %collective-permute-start.1 = (bf16[32,2,2,128]{3,2,1,0:T(2,128)(2,1)}, bf16[32,2,2,128]{3,2,1,0:T(2,128)(2,1)S(1)}, u32[]{:S(2)}, u32[]{:S(2)}) collective-permute-start(bf16[32,2,2,128]{3,2,1,0:T(2,128)(2,1)} %get-tuple-element.10), channel_id=1, source_target_pairs={{0,4},{4,0},{8,12},{12,8},{1,5},{5,1},{9,13},{13,9},{2,6},{6,2},{1... | collective-permute-start | bytes 98312 | tf_op jit(solution)/shard_map/ppermute | solution.py:765
  7.0 19.8 %collective-permute-start.5 = (bf16[192,2,2,128]{3,0,1,2:T(8,128)(2,1)S(1)}, bf16[192,2,2,128]{3,0,1,2:T(8,128)(2,1)S(1)}, u32[]{:S(2)}, u32[]{:S(2)}) collective-permute-start(bf16[192,2,2,128]{3,0,1,2:T(8,128)(2,1)S(1)} %copy.38), channel_id=1, source_target_pairs={{0,8},{4,12},{8,0},{12,4},{1,9},{5,13},{9,1},{13,5},{2,10},{6,14},... | collective-permute-start | bytes 589832 | tf_op jit(solution)/shard_map/ppermute | solution.py:762
  8.3 22.2 %collective-permute-start.4 = (bf16[192,2,2,128]{3,0,1,2:T(8,128)(2,1)S(1)}, bf16[192,2,2,128]{3,0,1,2:T(8,128)(2,1)S(1)}, u32[]{:S(2)}, u32[]{:S(2)}) collective-permute-start(bf16[192,2,2,128]{3,0,1,2:T(8,128)(2,1)S(1)} %copy.38), channel_id=1, source_target_pairs={{0,4},{4,0},{8,12},{12,8},{1,5},{5,1},{9,13},{13,9},{2,6},{6,2},{1... | collective-permute-start | bytes 589832 | tf_op jit(solution)/shard_map/ppermute | solution.py:765
  10.4 16.3 %collective-permute-start.2 = (bf16[144,2,128]{2,0,1:T(8,128)(2,1)S(1)}, bf16[144,2,128]{2,0,1:T(8,128)(2,1)S(1)}, u32[]{:S(2)}, u32[]{:S(2)}) collective-permute-start(bf16[144,2,128]{2,0,1:T(8,128)(2,1)S(1)} %pad_maximum_fusion), channel_id=1, source_target_pairs={{0,8},{4,12},{8,0},{12,4},{1,9},{5,13},{9,1},{13,5},{2,10},{6,14},... | collective-permute-start | bytes 221192 | tf_op jit(solution)/shard_map/ppermute | solution.py:762
  25.5 15.6 %collective-permute-start.8 = (bf16[2,768,128]{2,1,0:T(8,128)(2,1)S(1)}, bf16[2,768,128]{2,1,0:T(8,128)(2,1)S(1)}, u32[]{:S(2)}, u32[]{:S(2)}) collective-permute-start(bf16[2,768,128]{2,1,0:T(8,128)(2,1)S(1)} %shard_map.96), channel_id=1, source_target_pairs={{0,8},{4,12},{8,0},{12,4},{1,9},{5,13},{9,1},{13,5},{2,10},{6,14},... | collective-permute-start | bytes 1179656 | tf_op jit(solution)/shard_map/ppermute | solution.py:762
  26.8 3.7 %collective-permute-start.6 = (bf16[192,2,2,128]{3,0,1,2:T(8,128)(2,1)S(1)}, bf16[192,2,2,128]{3,0,1,2:T(8,128)(2,1)S(1)}, u32[]{:S(2)}, u32[]{:S(2)}) collective-permute-start(bf16[192,2,2,128]{3,0,1,2:T(8,128)(2,1)S(1)} %collective-permute-done.5), channel_id=1, source_target_pairs={{0,4},{4,0},{8,12},{12,8},{1,5},{5,1},{9,13},{13,9},{2,6},{6,2},{1... | collective-permute-start | bytes 589832 | tf_op jit(solution)/shard_map/ppermute | solution.py:765
  30.3 10.8 %collective-permute-start.9 = (bf16[2,232,128]{2,1,0:T(8,128)(2,1)S(1)}, bf16[2,232,128]{2,1,0:T(8,128)(2,1)S(1)}, u32[]{:S(2)}, u32[]{:S(2)}) collective-permute-start(bf16[2,232,128]{2,1,0:T(8,128)(2,1)S(1)} %shard_map.97), channel_id=1, source_target_pairs={{0,8},{4,12},{8,0},{12,4},{1,9},{5,13},{9,1},{13,5},{2,10},{6,14},... | collective-permute-start | bytes 356360 | tf_op jit(solution)/shard_map/ppermute | solution.py:762

commit v2 on v1

--- a/solution.py
+++ b/solution.py
@@ -443,7 +443,7 @@
             pltpu.SemaphoreType.DMA((2 + heads,)),
         ],
         compiler_params=pltpu.CompilerParams(
-            collective_id=0, has_side_effects=True, vmem_limit_bytes=56 * 2**20
+            collective_id=0, has_side_effects=True, vmem_limit_bytes=48 * 2**20
         ),
         name="combine",
     )(counts, queries, blob, prior)
@@ -559,41 +559,105 @@
             )
 
 
-def remote_kernel(rows_valid, queries, turned, partial, plain, scaled):
+def fill_tail(queries, steps, first, tail):
+    window = queries.shape[0] - first
+    count = steps.shape[0]
+    tail[...] = jnp.zeros_like(tail)
+    tail[pl.ds(0, window), :] = queries[pl.ds(first, window), :]
+    tail[pl.ds(window, count), :] = steps
+
+
+def rows_at(sizes, who, first):
+    n, _, group, tok_rows, step_count, _ = sizes
+    window_rows = tok_rows * group
+    at = first + lax.broadcasted_iota(jnp.int32, (TILE, 1), 0)
+    return jnp.where(
+        at < window_rows,
+        at + who * window_rows,
+        at + (n - 1) * window_rows + who * (step_count // n * group),
+    )
+
+
+def rows_scale(sizes, counts, position):
+    token = jnp.floor((position.astype(jnp.float32) + 0.5) / sizes[2])
+    place_in_prompt = token + (counts[0] + 1).astype(jnp.float32)
+    return 1.0 / (LANES * jnp.sqrt(place_in_prompt))
+
+
+def remote_kernel(
+    sizes, early, counts, queries, steps, turned, partial, tail, mixed, plain, scaled
+):
+    n, heads, rows_valid = sizes[0], sizes[1], sizes[5]
     first_offset, _ = chip_place(rows_valid)
-    count = partial.shape[1]
+    across = lax.rem(lax.axis_index("ctx") + 2, n)
+    there = lax.div(across, 2)
+    for head in range(heads):
+        turn_queries(
+            lambda at: queries[head, pl.ds(at, LANES), :], early, plain, scaled
+        )
+        for tile in range(early // TILE + 1):
+            first = tile * TILE
+            if first == early:
+                fill_tail(queries.at[head], steps[there, head], early, tail)
+                turn_queries(lambda at: tail[pl.ds(at, LANES), :], TILE, plain, scaled)
+            rows = carry_tile(
+                turned.at[head], first_offset, plain, scaled, tile if first < early else 0
+            )
+            rows = rows * rows_scale(sizes, counts, rows_at(sizes, across, first))
+            size = min(TILE, partial.shape[0] // heads - first)
+            mixed[pl.ds(first * heads + head, size, stride=heads), :] = rows[:size]
+    partial[...] = mixed[...].astype(partial.dtype)
+
+
+def merge_kernel(n, own, twin, send):
+    core = lax.rem(lax.axis_index("ctx"), 2)
+    step_count, rows, heads = own.shape[:3]
+    group = rows - heads
+    per_shard = step_count // n
+
+    def both(step, first, count):
+        at = (step, pl.ds(first, count))
+        return own[at] + twin[at]
+
+    for at in range(n // 2):
+        for step in range(per_shard):
+            row = (at * per_shard + step) * group
+            send[pl.ds(row, group)] = both((core + 2 * at) * per_shard + step, 0, group)
+    for step in range(step_count):
+        row = n // 2 * per_shard * group + step * heads
+        send[pl.ds(row, heads)] = both(step, group, heads)
+
+
+def own_tail_kernel(rows_valid, early, queries, steps, turned, local, tail, plain, scaled):
+    first_offset, _ = chip_place(rows_valid)
+    here = lax.div(lax.axis_index("ctx"), 2)
     for head in range(turned.shape[0]):
-        turn_queries(
-            lambda at: queries[head, pl.ds(at, LANES), :], count, plain, scaled
-        )
-        for tile in range(count // TILE):
-            partial[head, pl.ds(tile * TILE, TILE), :] = carry_tile(
-                turned.at[head], first_offset, plain, scaled, tile
-            ).astype(partial.dtype)
-
-
-def fill_tail(head, queries, steps, first, tail):
-    window = queries.shape[1] - first
-    count = steps.shape[1]
-    tail[...] = jnp.zeros_like(tail)
-    tail[pl.ds(0, window), :] = queries[head, pl.ds(first, window), :]
-    tail[pl.ds(window, count), :] = steps[head]
-
-
-def remote_tail_kernel(rows_valid, first, queries, steps, turned, partial, tail, plain, scaled):
-    first_offset, _ = chip_place(rows_valid)
-    for head in range(turned.shape[0]):
-        fill_tail(head, queries, steps, first, tail)
+        fill_tail(queries.at[head], steps[here, head], early, tail)
         turn_queries(lambda at: tail[pl.ds(at, LANES), :], TILE, plain, scaled)
-        rows = carry_tile(turned.at[head], first_offset, plain, scaled, 0)
-        partial[head] = rows[: partial.shape[1]].astype(partial.dtype)
+        local[head] = carry_tile(turned.at[head], first_offset, plain, scaled, 0)
+
+
+def finish_kernel(result, got, window_out, step_out, total, sems):
+    rows = window_out.shape[0]
+    total[...] = (result[...] + got[...].astype(jnp.float32)).astype(total.dtype)
+    copies = (
+        pltpu.make_async_copy(total.at[pl.ds(0, rows)], window_out, sems.at[0]),
+        pltpu.make_async_copy(
+            total.at[pl.ds(rows, total.shape[0] - rows)], step_out, sems.at[1]
+        ),
+    )
+    for copy in copies:
+        copy.start()
+    for copy in copies:
+        copy.wait()
 
 
 def late_kernel(
     sizes,
+    counts,
     queries,
     steps,
-    turned,
+    local_tail,
     local,
     own_pairs,
     twin_pairs,
@@ -604,8 +668,6 @@
     result,
     state_out,
     tail,
-    plain,
-    scaled,
     key_rows,
     value_rows,
     keys_plain,
@@ -615,12 +677,9 @@
     state_sem,
 ):
     n, heads, group, tok_rows, step_count, rows_valid = sizes
-    first_offset, _ = chip_place(rows_valid)
     me = lax.axis_index("ctx")
     twin = me + 1 - 2 * lax.rem(me, 2)
     window = n * tok_rows
-    window_rows = tok_rows * group
-    per_shard = step_count // n
     first_tail = local.shape[1]
     padded_keys = key_rows.shape[1]
     chunks = padded_keys // LANES
@@ -687,39 +746,75 @@
         state_copy(head).start()
 
     for head in range(heads):
-        fill_tail(head, queries, steps, first_tail, tail)
-        turn_queries(lambda at: tail[pl.ds(at, LANES), :], TILE, plain, scaled)
-        carried_tail = carry_tile(turned.at[head], first_offset, plain, scaled, 0)
-        for first in range(0, result.shape[1], TILE):
+        fill_tail(queries.at[head], steps[lax.div(me, 2), head], first_tail, tail)
+        rows_out = result.shape[0] // heads
+        for first in range(0, rows_out, TILE):
             last = first >= first_tail
             rows = tail[...] if last else queries[head, pl.ds(first, TILE), :]
             scores = lax.dot_general(
                 rows, key_rows[head], CONTRACT_LAST, preferred_element_type=jnp.float32
             )
-            at = first + lax.broadcasted_iota(jnp.int32, (TILE, 1), 0)
-            position = jnp.where(
-                at < window_rows,
-                at + me * window_rows,
-                at - window_rows + window * group + me * (per_shard * group),
-            )
+            position = rows_at(sizes, me, first)
             key_index = lax.broadcasted_iota(jnp.int32, scores.shape, 1)
             weights = jnp.where(position >= key_index * group, scores * scores, 0.0)
             total = jnp.dot(
                 weights.astype(jnp.bfloat16), value_rows[head], preferred_element_type=jnp.float32
             )
-            carried = carried_tail if last else local[head, pl.ds(first, TILE), :]
-            size = min(TILE, result.shape[1] - first)
-            result[head, pl.ds(first, size), :] = (total + carried)[:size]
+            carried = local_tail[head] if last else local[head, pl.ds(first, TILE), :]
+            size = min(TILE, rows_out - first)
+            total = (total + carried) * rows_scale(sizes, counts, position)
+            result[pl.ds(first * heads + head, size, stride=heads), :] = total[:size]
     for head in range(heads):
         state_copy(head).wait()
 
 
+def pick_both_kernel(ids_ref, query_table, pair_table, picked, query_sem, pair_sem):
+    vocab_rows, group = query_table.shape[:2]
+    first_row = lax.axis_index("ctx") * vocab_rows
+    heads = pair_table.shape[1]
+    picked[...] = jnp.zeros_like(picked)
+
+    def each(step, act):
+        row = ids_ref[step] - first_row
+
+        @pl.when(jnp.logical_and(row >= 0, row < vocab_rows))
+        def _():
+            to_queries = picked.at[step, pl.ds(0, group)]
+            to_pairs = picked.at[step, pl.ds(group, heads)]
+            act(pltpu.make_async_copy(query_table.at[row], to_queries, query_sem.at[step]))
+            act(pltpu.make_async_copy(pair_table.at[row], to_pairs, pair_sem.at[step]))
+
+    for step in range(picked.shape[0]):
+        each(step, lambda copy: copy.start())
+    for step in range(picked.shape[0]):
+        each(step, lambda copy: copy.wait())
+
+
+def pick_both(ids, query_table, pair_table):
+    steps, group, heads = ids.shape[0], query_table.shape[1], pair_table.shape[1]
+    shape = (steps, group + heads) + pair_table.shape[2:]
+    return pl.pallas_call(
+        pick_both_kernel,
+        out_shape=jax.ShapeDtypeStruct(shape, pair_table.dtype),
+        in_specs=[
+            pl.BlockSpec(memory_space=pltpu.SMEM),
+            pl.BlockSpec(memory_space=pl.ANY),
+            pl.BlockSpec(memory_space=pl.ANY),
+        ],
+        out_specs=pl.BlockSpec(memory_space=pltpu.VMEM),
+        scratch_shapes=[pltpu.SemaphoreType.DMA((steps,)), pltpu.SemaphoreType.DMA((steps,))],
+        compiler_params=pltpu.CompilerParams(vmem_limit_bytes=56 * 2**20),
+        name="pick_both",
+    )(ids, query_table, pair_table)
+
+
 def vmem_call(kernel, out_shape, operands, scratch, limit, out_specs=None):
+    smem = pl.BlockSpec(memory_space=pltpu.SMEM)
     vmem = pl.BlockSpec(memory_space=pltpu.VMEM)
     return pl.pallas_call(
         kernel,
         out_shape=out_shape,
-        in_specs=[vmem] * len(operands),
+        in_specs=[smem if operand.ndim == 1 else vmem for operand in operands],
         out_specs=out_specs if out_specs is not None else jax.tree.map(lambda _: vmem, out_shape),
         scratch_shapes=scratch,
         compiler_params=pltpu.CompilerParams(vmem_limit_bytes=limit * 2**20),
@@ -739,8 +834,6 @@
 ):
     tok_rows, heads, group, head_size = queries.shape
     n = lax.axis_size("ctx")
-    me = lax.axis_index("ctx")
-    core, chip = lax.rem(me, 2), lax.div(me, 2)
     step_count = continuation.shape[0]
     per_shard = step_count // n
     step_rows = per_shard * group
@@ -756,6 +849,7 @@
     )
     padded_keys = round_up(n * tok_rows + step_count, LANES)
     bf16, f32 = jnp.bfloat16, jnp.float32
+    sizes = (n, heads, group, tok_rows, step_count, rows_valid)
     shape = jax.ShapeDtypeStruct
 
     def swap_across(value):
@@ -774,24 +868,19 @@
     across_pairs = swap_across(keys_values)
     twin_prior = swap_twin(prior)
     twin_pairs = swap_twin(keys_values)
-    query_pick, pair_pick = pick_rows(
-        continuation, query_table.transpose(0, 2, 1, 3), pair_table
-    )
-    query_chip = query_pick + swap_twin(query_pick)
-    pair_chip = pair_pick + swap_twin(pair_pick)
-    mine = [
-        lax.dynamic_slice_in_dim(query_chip, (core + 2 * at) * per_shard, per_shard)
-        for at in range(n // 2)
-    ]
-    send = jnp.concatenate(
-        [part.reshape(step_rows, heads, head_size) for part in mine]
-        + [pair_chip.reshape(step_count * heads, 2, head_size)]
+    picked = pick_both(continuation, query_table.transpose(0, 2, 1, 3), pair_table)
+    twin_picked = swap_twin(picked)
+    send = vmem_call(
+        functools.partial(merge_kernel, n),
+        shape((n // 2 * step_rows + step_count * heads, 2, head_size), bf16),
+        (picked, twin_picked),
+        [],
+        4,
     )
     steps = send + swap_across(send)
     step_pairs = pair_planes(steps[n // 2 * step_rows :].reshape(step_count, heads, 2, head_size))
-    step_queries = steps[: n // 2 * step_rows].transpose(1, 0, 2)
-    own_steps = lax.dynamic_slice_in_dim(step_queries, chip * step_rows, step_rows, 1)
-    across_steps = lax.dynamic_slice_in_dim(step_queries, (1 - chip) * step_rows, step_rows, 1)
+    step_queries = steps[: n // 2 * step_rows].reshape(n // 2, step_rows, heads, head_size)
+    step_queries = step_queries.transpose(0, 2, 1, 3)
 
     own_rows = query_planes(queries)
     turned, local = vmem_call(
@@ -803,35 +892,38 @@
     )
     across_rows = query_planes(across_queries)
     partial = vmem_call(
-        functools.partial(remote_kernel, rows_valid),
-        shape((heads, early, LANES), bf16),
-        (across_rows, turned),
-        turn_scratch(early),
+        functools.partial(remote_kernel, sizes, early),
+        shape((heads * (window_rows + step_rows), LANES), bf16),
+        (counts, across_rows, step_queries, turned),
+        [
+            pltpu.VMEM((TILE, LANES), bf16),
+            pltpu.VMEM((heads * (window_rows + step_rows), LANES), f32),
+        ]
+        + turn_scratch(early),
         16,
     )
     got = swap_across(partial)
-    partial_tail = vmem_call(
-        functools.partial(remote_tail_kernel, rows_valid, early),
-        shape((heads, window_rows - early + step_rows, LANES), bf16),
-        (across_rows, across_steps, turned),
+    far_pairs = swap_twin(across_pairs)
+    local_tail = vmem_call(
+        functools.partial(own_tail_kernel, rows_valid, early),
+        shape((heads, TILE, LANES), f32),
+        (own_rows, step_queries, turned),
         [pltpu.VMEM((TILE, LANES), bf16)] + turn_scratch(TILE),
         16,
     )
-    got_tail = swap_across(partial_tail)
-    far_pairs = swap_twin(across_pairs)
-    sizes = (n, heads, group, tok_rows, step_count, rows_valid)
     vmem = pl.BlockSpec(memory_space=pltpu.VMEM)
     chunks = padded_keys // LANES
     result, decode_state = vmem_call(
         functools.partial(late_kernel, sizes),
         (
-            shape((heads, window_rows + step_rows, LANES), f32),
+            shape((heads * (window_rows + step_rows), LANES), f32),
             shape((heads, rows_valid, LANES), f32),
         ),
         (
+            counts,
             own_rows,
-            own_steps,
-            turned,
+            step_queries,
+            local_tail,
             local,
             pair_planes(keys_values),
             pair_planes(twin_pairs),
@@ -840,9 +932,8 @@
             step_pairs,
             prior,
         ),
-        [pltpu.VMEM((TILE, LANES), bf16)]
-        + turn_scratch(TILE)
-        + [
+        [
+            pltpu.VMEM((TILE, LANES), bf16),
             pltpu.VMEM((heads, padded_keys, LANES), bf16),
             pltpu.VMEM((heads, padded_keys, LANES), bf16),
             pltpu.VMEM((chunks, LANES, LANES), f32),
@@ -854,15 +945,18 @@
         24,
         (vmem, pl.BlockSpec(memory_space=pl.ANY)),
     )
-    window_at = counts[0] + 1 + me * tok_rows + jnp.arange(window_rows, dtype=jnp.int32) // group
-    steps_at = counts[0] + 1 + n * tok_rows + me * per_shard
-    steps_at = steps_at + jnp.arange(step_rows, dtype=jnp.int32) // group
-    scale = 1.0 / (head_size * jnp.sqrt(jnp.concatenate([window_at, steps_at]).astype(f32)))
-    total = result + jnp.concatenate([got, got_tail], axis=1).astype(f32)
-    total = (total * scale[None, :, None]).astype(bf16)
-    readout = total[:, :window_rows].reshape(heads, tok_rows, group, head_size)
-    decode_out = total[:, window_rows:].reshape(heads, per_shard, group, head_size)
-    return (readout.transpose(1, 0, 2, 3), decode_out.transpose(1, 0, 2, 3), decode_state)
+    hbm = pl.BlockSpec(memory_space=pl.ANY)
+    readout, decode_out = vmem_call(
+        finish_kernel,
+        (shape((heads * window_rows, LANES), bf16), shape((heads * step_rows, LANES), bf16)),
+        (result, got),
+        [pltpu.VMEM(got.shape, bf16), pltpu.SemaphoreType.DMA((2,))],
+        8,
+        (hbm, hbm),
+    )
+    readout = readout.reshape(tok_rows, group, heads, head_size)
+    decode_out = decode_out.reshape(per_shard, group, heads, head_size)
+    return (readout.transpose(0, 2, 1, 3), decode_out.transpose(0, 2, 1, 3), decode_state)
 
 
 def solution(mesh):

time: 43.6 us -> 59.7 us (1.37)
  waiting for transfers between devices: 3.66 us -> 22.1 us
  Pallas kernels: 24.2 us -> 26.9 us
  other arithmetic: 2.18 us -> 0.08 us
  local copies, waits for them, and re-layouts: 3.25 us -> 1.15 us
  starting transfers between devices: 8.47 us -> 7.71 us
    ppermute x5 -> x4, waiting for transfers between devices: 3.2 us -> 20.9 us  [swap_across(): return lax.ppermute(value, 'ctx', [(i, (i + 2) % n) for i in range(n)])]
    pallas_call x5 -> x7, Pallas kernels: 24.2 us -> 26.9 us  [the longest x6 24 us: vmem_call(): pl.pallas_call(kernel, out_shape=out_shape, in_specs=[smem if operand.ndi...]
    slice x5 -> x1, local copies, waits for them, and re-layouts: 1.95 us -> 0.03 us  [on_device_exchange(): steps[:n // 2 * step_rows].reshape(n // 2, step_rows, heads, head_size)]
    add x4 -> x0, other arithmetic: 1.83 us -> none  [the longest x1 1.02 us: on_device_exchange(): query_chip = query_pick + swap_twin(query_pick)]
    ppermute x5 -> x4, starting transfers between devices: 5.74 us -> 4.35 us  [swap_across(): return lax.ppermute(value, 'ctx', [(i, (i + 2) % n) for i in range(n)])]
    reshape x2, local copies, waits for them, and re-layouts: 1.16 us -> 0.13 us  [query_planes(): return value.transpose(1, 0, 2, 3).reshape(heads, -1, head_size)]
    unnamed x7 -> x9, local copies, waits for them, and re-layouts: 0.04 us -> 0.94 us
    ppermute x5 -> x4, waiting for transfers between devices: 0.46 us -> 1.18 us  [swap_twin(): return lax.ppermute(value, 'ctx', [(i, i ^ 1) for i in range(n)])]
  transfers between devices with their start and end apart: 10 -> 8, of which waited for: 2 -> 3; matrix products, arithmetic and copies ran while one was open for 7% -> 1% of each run, Pallas kernels for 56% -> 23%
where the time goes in v2:
time: 59.7 us; the launch traced here: 59.5 us
  Pallas kernels  26.9 us (45%)
  waiting for transfers between devices  22.1 us (37%)
  starting transfers between devices  7.71 us (13%)
  between operations  1.62 us (3%)
  local copies, waits for them, and re-layouts  1.15 us (2%)
    pallas_call x6, Pallas kernels, vmem_call(): pl.pallas_call(kernel, out_shape=out_shape, in_specs=[smem if operand.ndi...  24 us
    ppermute x4, waiting for transfers between devices, swap_across(): return lax.ppermute(value, 'ctx', [(i, (i + 2) % n) for i in range(n)])  20.9 us
    ppermute x4, starting transfers between devices, swap_across(): return lax.ppermute(value, 'ctx', [(i, (i + 2) % n) for i in range(n)])  4.35 us
    ppermute x4, starting transfers between devices, swap_twin(): return lax.ppermute(value, 'ctx', [(i, i ^ 1) for i in range(n)])  3.35 us
    pallas_call x1, Pallas kernels, pick_both(): pl.pallas_call(pick_both_kernel, out_shape=jax.ShapeDtypeStruct(shape, pa...  2.89 us
  transfers between devices with their start and end apart: 8, of which 3 were waited for; matrix products, arithmetic and copies ran while one was open for 1% of the time, Pallas kernels for 23%

profile of v2, /device:TPU:1, one launch (start us, length us, event | category | flops | bytes accessed | tf_op | source)
XLA Modules:
  0.0 59.5 jit_solution(2158860937792534072)
XLA Ops:
  0.6 0.1 collective-permute-start.2
  0.7 2.7 %collective-permute-start.6 = (bf16[192,2,5,128]{3,1,2,0:T(2,128)(2,1)}, bf16[192,2,5,128]{3,1,2,0:T(2,128)(2,1)S(1)}, u32[]{:S(2)}, u32[]{:S(2)}) collective-permute-start(bf16[192,2,5,128]{3,1,2,0:T(2,128)(2,1)} %param.7), channel_id=1, source_target_pairs={{0,8},{4,12},{8,0},{12,4},{1,9},{5,13},{9,1},{13,5},{2,10},{6,14},... | collective-permute-start | bytes 1474568 | tf_op jit(solution)/shard_map/ppermute | solution.py:856
  3.4 0.0 copy-start.2
  3.4 2.9 %pick_both.1.own = bf16[32,7,2,128]{3,2,1,0:T(2,128)(2,1)} custom-call(s32[32]{0:T(128)} %ids_ref.1, bf16[18992,5,2,128]{3,2,1,0:T(2,128)(2,1)} %bitcast.34, bf16[18992,2,2,128]{3,2,1,0:T(2,128)(2,1)} %pair_table.1), custom_call_target="tpu_custom_call" | custom-call | tf_op jit(solution)/shard_map/pick_both/pallas_call | solution.py:796
  6.3 0.0 copy-start
  6.3 0.5 collective-permute-start
  6.9 1.2 %collective-permute-done.twin = bf16[32,7,2,128]{3,2,1,0:T(2,128)(2,1)S(1)} collective-permute-done((bf16[32,7,2,128]{3,2,1,0:T(2,128)(2,1)}, bf16[32,7,2,128]{3,2,1,0:T(2,128)(2,1)S(1)}, u32[]{:S(2)}, u32[]{:S(2)}) %collective-permute-start) | collective-permute-done | bytes 114720 | tf_op jit(solution)/shard_map/ppermute | solution.py:859
  8.0 0.0 copy-start.1
  8.0 0.9 %copy-done.1 = bf16[32,7,2,128]{3,2,1,0:T(2,128)(2,1)S(1)} copy-done((bf16[32,7,2,128]{3,2,1,0:T(2,128)(2,1)S(1)}, bf16[32,7,2,128]{3,2,1,0:T(2,128)(2,1)}, u32[]{:S(2)}) %copy-start.1) | copy-done | bytes 114712
  8.9 0.1 shard_map.94
  9.0 0.1 collective-permute-start.1
  9.7 0.0 copy-done.2
  9.7 0.1 copy.24.queries
  9.8 6.9 %collective-permute-done.1 = bf16[144,2,128]{2,1,0:T(2,128)(2,1)S(1)} collective-permute-done((bf16[144,2,128]{2,1,0:T(2,128)(2,1)S(1)}, bf16[144,2,128]{2,1,0:T(2,128)(2,1)S(1)}, u32[]{:S(2)}, u32[]{:S(2)}) %collective-permute-start.1) | collective-permute-done | bytes 73760 | tf_op jit(solution)/shard_map/ppermute | solution.py:856
  16.7 0.1 add.3
  16.8 0.0 collective-permute-done.6
  16.9 0.1 copy.25.queries
  16.9 0.0 collective-permute-done.2.other
  16.9 0.0 copy-done
  17.0 5.0 %shard_map.95 = (bf16[2,128,4224]{2,1,0:T(8,128)(2,1)S(1)}, f32[2,768,128]{2,1,0:T(8,128)S(1)}) custom-call(bf16[2,960,128]{2,1,0:T(8,128)(2,1)S(1)} %copy.24.queries, bf16[2,2064,128]{2,1,0:T(8,128)(2,1)S(1)} %copy-done, bf16[2,2064,128]{2,1,0:T(8,128)(2,1)S(1)} %collective-permute-done.2.other), custom_call_target="tpu_custom_call" | custom-call | tf_op jit(solution)/shard_map/pallas_call | solution.py:814
  22.0 0.0 copy-start.3
  22.0 7.0 %shard_map.98 = bf16[2000,128]{1,0:T(8,128)(2,1)S(1)} custom-call(s32[1]{0:T(128)S(6)} %copy.37.counts, bf16[2,960,128]{2,1,0:T(8,128)(2,1)S(1)} %copy.25.queries, bf16[2,2,40,128]{3,2,1,0:T(8,128)(2,1)S(1)} %bitcast.27, bf16[2,128,4224]{2,1,0:T(8,128)(2,1)S(1)} %get-tuple-element.9.turned), custom_call_target="tpu_custom_call" | custom-call | tf_op jit(solution)/shard_map/pallas_call | solution.py:814
  29.0 1.2 %collective-permute-start.7 = (bf16[2000,128]{1,0:T(8,128)(2,1)S(1)}, bf16[2000,128]{1,0:T(8,128)(2,1)S(1)}, u32[]{:S(2)}, u32[]{:S(2)}) collective-permute-start(bf16[2000,128]{1,0:T(8,128)(2,1)S(1)} %shard_map.98), channel_id=1, source_target_pairs={{0,8},{4,12},{8,0},{12,4},{1,9},{5,13},{9,1},{13,5},{2,10},{6,14},... | collective-permute-start | bytes 1536008 | tf_op jit(solution)/shard_map/ppermute | solution.py:856
  30.3 0.0 copy-done.3
  30.3 0.3 collective-permute-start.4
  30.7 1.2 %collective-permute-start.3 = (bf16[192,2,2,128]{3,0,1,2:T(8,128)(2,1)S(1)}, bf16[192,2,2,128]{3,0,1,2:T(8,128)(2,1)S(1)}, u32[]{:S(2)}, u32[]{:S(2)}) collective-permute-start(bf16[192,2,2,128]{3,0,1,2:T(8,128)(2,1)S(1)} %copy.36), channel_id=1, source_target_pairs={{0,4},{4,0},{8,12},{12,8},{1,5},{5,1},{9,13},{13,9},{2,6},{6,2},{1... | collective-permute-start | bytes 589832 | tf_op jit(solution)/shard_map/ppermute | solution.py:859
  31.9 14.0 %collective-permute-done.4 = bf16[192,2,2,128]{3,0,1,2:T(8,128)(2,1)S(1)} collective-permute-done((bf16[192,2,2,128]{3,0,1,2:T(8,128)(2,1)S(1)}, bf16[192,2,2,128]{3,0,1,2:T(8,128)(2,1)S(1)}, u32[]{:S(2)}, u32[]{:S(2)}) %collective-permute-start.4) | collective-permute-done | bytes 196640 | tf_op jit(solution)/shard_map/ppermute | solution.py:856
  45.9 1.5 %collective-permute-start.5 = (bf16[192,2,2,128]{3,0,1,2:T(8,128)(2,1)S(1)}, bf16[192,2,2,128]{3,0,1,2:T(8,128)(2,1)S(1)}, u32[]{:S(2)}, u32[]{:S(2)}) collective-permute-start(bf16[192,2,2,128]{3,0,1,2:T(8,128)(2,1)S(1)} %collective-permute-done.4), channel_id=1, source_target_pairs={{0,4},{4,0},{8,12},{12,8},{1,5},{5,1},{9,13},{13,9},{2,6},{6,2},{1... | collective-permute-start | bytes 589832 | tf_op jit(solution)/shard_map/ppermute | solution.py:859
  47.4 1.8 %shard_map.96.local_tail = f32[2,256,128]{2,1,0:T(8,128)S(1)} custom-call(bf16[2,960,128]{2,1,0:T(8,128)(2,1)S(1)} %copy.24.queries, bf16[2,2,40,128]{3,2,1,0:T(8,128)(2,1)S(1)} %bitcast.28, bf16[2,128,4224]{2,1,0:T(8,128)(2,1)S(1)} %get-tuple-element.9.turned), custom_call_target="tpu_custom_call" | custom-call | tf_op jit(solution)/shard_map/pallas_call | solution.py:814
  49.3 0.0 collective-permute-done.3
  49.3 0.0 collective-permute-done.5
  49.3 9.1 %shard_map.97 = (f32[2000,128]{1,0:T(8,128)S(1)}, f32[2,2064,128]{2,1,0:T(8,128)}) custom-call(s32[1]{0:T(128)S(6)} %copy.37.counts, bf16[2,960,128]{2,1,0:T(8,128)(2,1)S(1)} %copy.24.queries, bf16[2,2,40,128]{3,2,1,0:T(8,128)(2,1)S(1)} %bitcast.29, f32[2,256,128]{2,1,0:T(8,128)S(1)} %shard_map.96.local_tail, f32[2,768,128]{2,1,0:T(8,128)S(1)} %get-tuple-element.10.local, ...), custom_call_target="tpu_custom_call" | custom-call | tf_op jit(solution)/shard_map/pallas_call | solution.py:814
  58.4 0.0 collective-permute-done.7.got
  58.5 0.9 %shard_map.99 = (bf16[1920,128]{1,0:T(8,128)(2,1)}, bf16[80,128]{1,0:T(8,128)(2,1)}) custom-call(f32[2000,128]{1,0:T(8,128)S(1)} %get-tuple-element.11.result, bf16[2000,128]{1,0:T(8,128)(2,1)S(1)} %collective-permute-done.7.got), custom_call_target="tpu_custom_call" | custom-call | tf_op jit(solution)/shard_map/pallas_call | solution.py:814
  (5 shorter events, 0.1 us)
Async XLA Ops:
  0.6 16.3 %collective-permute-start.2 = (bf16[2,2064,128]{2,1,0:T(8,128)(2,1)}, bf16[2,2064,128]{2,1,0:T(8,128)(2,1)S(1)}, u32[]{:S(2)}, u32[]{:S(2)}) collective-permute-start(bf16[2,2064,128]{2,1,0:T(8,128)(2,1)} %prior.1), channel_id=1, source_target_pairs={{0,4},{4,0},{8,12},{12,8},{1,5},{5,1},{9,13},{13,9},{2,6},{6,2},{1... | collective-permute-start | bytes 3170312 | tf_op jit(solution)/shard_map/ppermute | solution.py:859
  0.7 16.1 %collective-permute-start.6 = (bf16[192,2,5,128]{3,1,2,0:T(2,128)(2,1)}, bf16[192,2,5,128]{3,1,2,0:T(2,128)(2,1)S(1)}, u32[]{:S(2)}, u32[]{:S(2)}) collective-permute-start(bf16[192,2,5,128]{3,1,2,0:T(2,128)(2,1)} %param.7), channel_id=1, source_target_pairs={{0,8},{4,12},{8,0},{12,4},{1,9},{5,13},{9,1},{13,5},{2,10},{6,14},... | collective-permute-start | bytes 1474568 | tf_op jit(solution)/shard_map/ppermute | solution.py:856
  3.4 6.3 %copy-start.2 = (bf16[192,2,5,128]{3,1,2,0:T(2,128)(2,1)S(1)}, bf16[192,2,5,128]{3,1,2,0:T(2,128)(2,1)}, u32[]{:S(2)}) copy-start(bf16[192,2,5,128]{3,1,2,0:T(2,128)(2,1)} %param.7) | copy-start | bytes 1474564
  6.3 10.6 %copy-start = (bf16[2,2064,128]{2,1,0:T(8,128)(2,1)S(1)}, bf16[2,2064,128]{2,1,0:T(8,128)(2,1)}, u32[]{:S(2)}) copy-start(bf16[2,2064,128]{2,1,0:T(8,128)(2,1)} %prior.1) | copy-start | bytes 3170308
  6.3 1.7 %collective-permute-start = (bf16[32,7,2,128]{3,2,1,0:T(2,128)(2,1)}, bf16[32,7,2,128]{3,2,1,0:T(2,128)(2,1)S(1)}, u32[]{:S(2)}, u32[]{:S(2)}) collective-permute-start(bf16[32,7,2,128]{3,2,1,0:T(2,128)(2,1)} %pick_both.1.own), channel_id=1, source_target_pairs={{0,4},{4,0},{8,12},{12,8},{1,5},{5,1},{9,13},{13,9},{2,6},{6,2},{1... | collective-permute-start | bytes 344072 | tf_op jit(solution)/shard_map/ppermute | solution.py:859
  8.0 0.9 %copy-start.1 = (bf16[32,7,2,128]{3,2,1,0:T(2,128)(2,1)S(1)}, bf16[32,7,2,128]{3,2,1,0:T(2,128)(2,1)}, u32[]{:S(2)}) copy-start(bf16[32,7,2,128]{3,2,1,0:T(2,128)(2,1)} %pick_both.1.own) | copy-start | bytes 344068
  9.0 7.7 %collective-permute-start.1 = (bf16[144,2,128]{2,1,0:T(2,128)(2,1)S(1)}, bf16[144,2,128]{2,1,0:T(2,128)(2,1)S(1)}, u32[]{:S(2)}, u32[]{:S(2)}) collective-permute-start(bf16[144,2,128]{2,1,0:T(2,128)(2,1)S(1)} %shard_map.94), channel_id=1, source_target_pairs={{0,8},{4,12},{8,0},{12,4},{1,9},{5,13},{9,1},{13,5},{2,10},{6,14},... | collective-permute-start | bytes 221192 | tf_op jit(solution)/shard_map/ppermute | solution.py:856
  22.0 8.3 %copy-start.3 = (bf16[192,2,2,128]{3,2,1,0:T(2,128)(2,1)S(1)}, bf16[192,2,2,128]{3,2,1,0:T(2,128)(2,1)}, u32[]{:S(2)}) copy-start(bf16[192,2,2,128]{3,2,1,0:T(2,128)(2,1)} %param.8) | copy-start | bytes 589828
  29.0 29.4 %collective-permute-start.7 = (bf16[2000,128]{1,0:T(8,128)(2,1)S(1)}, bf16[2000,128]{1,0:T(8,128)(2,1)S(1)}, u32[]{:S(2)}, u32[]{:S(2)}) collective-permute-start(bf16[2000,128]{1,0:T(8,128)(2,1)S(1)} %shard_map.98), channel_id=1, source_target_pairs={{0,8},{4,12},{8,0},{12,4},{1,9},{5,13},{9,1},{13,5},{2,10},{6,14},... | collective-permute-start | bytes 1536008 | tf_op jit(solution)/shard_map/ppermute | solution.py:856
  30.3 15.6 %collective-permute-start.4 = (bf16[192,2,2,128]{3,0,1,2:T(8,128)(2,1)S(1)}, bf16[192,2,2,128]{3,0,1,2:T(8,128)(2,1)S(1)}, u32[]{:S(2)}, u32[]{:S(2)}) collective-permute-start(bf16[192,2,2,128]{3,0,1,2:T(8,128)(2,1)S(1)} %copy.36), channel_id=1, source_target_pairs={{0,8},{4,12},{8,0},{12,4},{1,9},{5,13},{9,1},{13,5},{2,10},{6,14},... | collective-permute-start | bytes 589832 | tf_op jit(solution)/shard_map/ppermute | solution.py:856
  30.7 18.6 %collective-permute-start.3 = (bf16[192,2,2,128]{3,0,1,2:T(8,128)(2,1)S(1)}, bf16[192,2,2,128]{3,0,1,2:T(8,128)(2,1)S(1)}, u32[]{:S(2)}, u32[]{:S(2)}) collective-permute-start(bf16[192,2,2,128]{3,0,1,2:T(8,128)(2,1)S(1)} %copy.36), channel_id=1, source_target_pairs={{0,4},{4,0},{8,12},{12,8},{1,5},{5,1},{9,13},{13,9},{2,6},{6,2},{1... | collective-permute-start | bytes 589832 | tf_op jit(solution)/shard_map/ppermute | solution.py:859
  45.9 3.4 %collective-permute-start.5 = (bf16[192,2,2,128]{3,0,1,2:T(8,128)(2,1)S(1)}, bf16[192,2,2,128]{3,0,1,2:T(8,128)(2,1)S(1)}, u32[]{:S(2)}, u32[]{:S(2)}) collective-permute-start(bf16[192,2,2,128]{3,0,1,2:T(8,128)(2,1)S(1)} %collective-permute-done.4), channel_id=1, source_target_pairs={{0,4},{4,0},{8,12},{12,8},{1,5},{5,1},{9,13},{13,9},{2,6},{6,2},{1... | collective-permute-start | bytes 589832 | tf_op jit(solution)/shard_map/ppermute | solution.py:859

commit v3 on v2

--- a/solution.py
+++ b/solution.py
@@ -584,28 +584,47 @@
     return 1.0 / (LANES * jnp.sqrt(place_in_prompt))
 
 
-def remote_kernel(
-    sizes, early, counts, queries, steps, turned, partial, tail, mixed, plain, scaled
+def send_tile(sizes, counts, head, first, rows, mixed, base):
+    n, heads = sizes[:2]
+    across = lax.rem(lax.axis_index("ctx") + 2, n)
+    rows = rows * rows_scale(sizes, counts, rows_at(sizes, across, first))
+    size = min(TILE, mixed.shape[0] // heads - (first - base))
+    mixed[pl.ds((first - base) * heads + head, size, stride=heads), :] = rows[:size]
+
+
+def remote_kernel(sizes, counts, queries, turned, partial, mixed, plain, scaled):
+    heads, rows_valid = sizes[1], sizes[5]
+    first_offset, _ = chip_place(rows_valid)
+    count = partial.shape[0] // heads
+    for head in range(heads):
+        turn_queries(
+            lambda at: queries[head, pl.ds(at, LANES), :], count, plain, scaled
+        )
+        for tile in range(count // TILE):
+            rows = carry_tile(turned.at[head], first_offset, plain, scaled, tile)
+            send_tile(sizes, counts, head, tile * TILE, rows, mixed, 0)
+    partial[...] = mixed[...].astype(partial.dtype)
+
+
+def remote_tail_kernel(
+    sizes, base, early, counts, queries, steps, turned, partial, tail, mixed, plain, scaled
 ):
     n, heads, rows_valid = sizes[0], sizes[1], sizes[5]
     first_offset, _ = chip_place(rows_valid)
-    across = lax.rem(lax.axis_index("ctx") + 2, n)
-    there = lax.div(across, 2)
+    there = lax.div(lax.rem(lax.axis_index("ctx") + 2, n), 2)
     for head in range(heads):
         turn_queries(
-            lambda at: queries[head, pl.ds(at, LANES), :], early, plain, scaled
-        )
-        for tile in range(early // TILE + 1):
-            first = tile * TILE
-            if first == early:
-                fill_tail(queries.at[head], steps[there, head], early, tail)
-                turn_queries(lambda at: tail[pl.ds(at, LANES), :], TILE, plain, scaled)
+            lambda at: queries[head, pl.ds(base + at, LANES), :], early - base, plain, scaled
+        )
+        for first in range(base, early, TILE):
             rows = carry_tile(
-                turned.at[head], first_offset, plain, scaled, tile if first < early else 0
+                turned.at[head], first_offset, plain, scaled, (first - base) // TILE
             )
-            rows = rows * rows_scale(sizes, counts, rows_at(sizes, across, first))
-            size = min(TILE, partial.shape[0] // heads - first)
-            mixed[pl.ds(first * heads + head, size, stride=heads), :] = rows[:size]
+            send_tile(sizes, counts, head, first, rows, mixed, base)
+        fill_tail(queries.at[head], steps[there, head], early, tail)
+        turn_queries(lambda at: tail[pl.ds(at, LANES), :], TILE, plain, scaled)
+        rows = carry_tile(turned.at[head], first_offset, plain, scaled, 0)
+        send_tile(sizes, counts, head, early, rows, mixed, base)
     partial[...] = mixed[...].astype(partial.dtype)
 
 
@@ -637,9 +656,11 @@
         local[head] = carry_tile(turned.at[head], first_offset, plain, scaled, 0)
 
 
-def finish_kernel(result, got, window_out, step_out, total, sems):
+def finish_kernel(result, got, got_tail, window_out, step_out, total, sems):
     rows = window_out.shape[0]
-    total[...] = (result[...] + got[...].astype(jnp.float32)).astype(total.dtype)
+    for part, first in ((got, 0), (got_tail, got.shape[0])):
+        at = pl.ds(first, part.shape[0])
+        total[at, :] = (result[at, :] + part[...].astype(jnp.float32)).astype(total.dtype)
     copies = (
         pltpu.make_async_copy(total.at[pl.ds(0, rows)], window_out, sems.at[0]),
         pltpu.make_async_copy(
@@ -650,6 +671,48 @@
         copy.start()
     for copy in copies:
         copy.wait()
+
+
+def state_blocks(load_keys, chunks, values, delta, keys_plain, keys_scaled, my_offset):
+    for chunk in range(chunks):
+        piece = turned_rows(load_keys(chunk))
+        twice = piece * ROOT_TWO
+        keys_plain[chunk] = piece
+        keys_scaled[chunk, pl.ds(0, LANES), :] = twice
+        keys_scaled[chunk, pl.ds(LANES, LANES), :] = twice
+
+    def key_features(block):
+        pieces = []
+        for chunk in range(chunks):
+            here = keys_plain[chunk]
+            other = keys_scaled[chunk, pl.ds(my_offset + block, LANES), :]
+            if block == 0:
+                other = jnp.where(my_offset == 0, here, other)
+            pieces.append((here * other).astype(jnp.bfloat16))
+        return jnp.concatenate(pieces, axis=1)
+
+    for block in range(delta.shape[0] // LANES):
+        delta[pl.ds(block * LANES, LANES), :] = jnp.dot(
+            key_features(block), values, preferred_element_type=jnp.float32
+        )
+
+
+def part_kernel(sizes, own_pairs, twin_pairs, delta, keys, values, keys_plain, keys_scaled):
+    heads, tok_rows, rows_valid = sizes[1], sizes[3], sizes[5]
+    my_offset = lax.div(lax.axis_index("ctx") * rows_valid, LANES)
+    for head in range(heads):
+        for plane, target in ((0, keys), (1, values)):
+            target[pl.ds(0, tok_rows), :] = own_pairs[plane, head]
+            target[pl.ds(tok_rows, tok_rows), :] = twin_pairs[plane, head]
+        state_blocks(
+            lambda chunk: keys[pl.ds(chunk * LANES, LANES), :],
+            keys.shape[0] // LANES,
+            values[...],
+            delta.at[head],
+            keys_plain,
+            keys_scaled,
+            my_offset,
+        )
 
 
 def late_kernel(
@@ -665,6 +728,7 @@
     far_pairs,
     step_pairs,
     prior,
+    part,
     result,
     state_out,
     tail,
@@ -682,8 +746,6 @@
     window = n * tok_rows
     first_tail = local.shape[1]
     padded_keys = key_rows.shape[1]
-    chunks = padded_keys // LANES
-    blocks = delta.shape[0] // LANES
     my_first = me * rows_valid
     my_offset = lax.div(my_first, LANES)
     my_lead = pl.multiple_of(lax.rem(my_first, LANES), 8)
@@ -708,41 +770,29 @@
                 target[head, pl.ds(window + step_count, spare), :] = jnp.zeros(
                     (spare, LANES), target.dtype
                 )
-        for chunk in range(chunks):
-            piece = turned_rows(key_rows[head, pl.ds(chunk * LANES, LANES), :])
-            twice = piece * ROOT_TWO
-            keys_plain[chunk] = piece
-            keys_scaled[chunk, pl.ds(0, LANES), :] = twice
-            keys_scaled[chunk, pl.ds(LANES, LANES), :] = twice
-
-        def key_features(block, maybe_plain):
-            pieces = []
-            for chunk in range(chunks):
-                here = keys_plain[chunk]
-                other = keys_scaled[chunk, pl.ds(my_offset + block, LANES), :]
-                if maybe_plain:
-                    other = jnp.where(my_offset == 0, here, other)
-                pieces.append((here * other).astype(jnp.bfloat16))
-            return jnp.concatenate(pieces, axis=1)
-
-        def add_block(features, first):
-            delta[pl.ds(first, features.shape[0]), :] = jnp.dot(
-                features, value_rows[head], preferred_element_type=jnp.float32
-            )
-
-        odd = 1 if blocks % 2 else 2
-        for block in range(odd):
-            add_block(key_features(block, block == 0), block * LANES)
-
-        @pl.loop(0, (blocks - odd) // 2)
-        def _(pair):
-            block = odd + 2 * pair
-            both = jnp.concatenate(
-                [key_features(block, False), key_features(block + 1, False)], axis=0
-            )
-            add_block(both, pl.multiple_of(block * LANES, LANES))
-
-        state[head] = prior[head].astype(jnp.float32) + delta[pl.ds(my_lead, rows_valid), :]
+        chip_rows = 2 * tok_rows
+        far = pl.multiple_of((1 - lax.div(me, 2)) * chip_rows, LANES)
+        chip_chunks = chip_rows // LANES
+        last = padded_keys - n * tok_rows
+
+        def load_keys(chunk):
+            first = far if chunk < chip_chunks else window - chip_rows
+            return key_rows[head, pl.ds(first + chunk * LANES, LANES), :]
+
+        values = jnp.concatenate(
+            [value_rows[head, pl.ds(far, chip_rows), :], value_rows[head, pl.ds(window, last), :]]
+        )
+        state_blocks(
+            load_keys,
+            (chip_rows + last) // LANES,
+            values,
+            delta,
+            keys_plain,
+            keys_scaled,
+            my_offset,
+        )
+        mine = pl.ds(my_lead, rows_valid)
+        state[head] = prior[head].astype(jnp.float32) + part[head, mine, :] + delta[mine, :]
         state_copy(head).start()
 
     for head in range(heads):
@@ -890,19 +940,40 @@
         [pltpu.VMEM((padded, LANES), bf16)] + turn_scratch(early),
         16,
     )
+    own_planes, twin_planes = pair_planes(keys_values), pair_planes(twin_pairs)
+    chip_chunks = 2 * tok_rows // LANES
+    part = vmem_call(
+        functools.partial(part_kernel, sizes),
+        shape((heads, blocks * LANES, LANES), f32),
+        (own_planes, twin_planes),
+        [
+            pltpu.VMEM((2 * tok_rows, LANES), bf16),
+            pltpu.VMEM((2 * tok_rows, LANES), bf16),
+            pltpu.VMEM((chip_chunks, LANES, LANES), f32),
+            pltpu.VMEM((chip_chunks, 2 * LANES, LANES), f32),
+        ],
+        16,
+    )
     across_rows = query_planes(across_queries)
+    half = (early // TILE + 1) // 2 * TILE
     partial = vmem_call(
-        functools.partial(remote_kernel, sizes, early),
-        shape((heads * (window_rows + step_rows), LANES), bf16),
+        functools.partial(remote_kernel, sizes),
+        shape((heads * half, LANES), bf16),
+        (counts, across_rows, turned),
+        [pltpu.VMEM((heads * half, LANES), f32)] + turn_scratch(half),
+        16,
+    )
+    got = swap_across(partial)
+    rest = heads * (window_rows + step_rows - half)
+    partial_tail = vmem_call(
+        functools.partial(remote_tail_kernel, sizes, half, early),
+        shape((rest, LANES), bf16),
         (counts, across_rows, step_queries, turned),
-        [
-            pltpu.VMEM((TILE, LANES), bf16),
-            pltpu.VMEM((heads * (window_rows + step_rows), LANES), f32),
-        ]
-        + turn_scratch(early),
+        [pltpu.VMEM((TILE, LANES), bf16), pltpu.VMEM((rest, LANES), f32)]
+        + turn_scratch(max(early - half, TILE)),
         16,
     )
-    got = swap_across(partial)
+    got_tail = swap_across(partial_tail)
     far_pairs = swap_twin(across_pairs)
     local_tail = vmem_call(
         functools.partial(own_tail_kernel, rows_valid, early),
@@ -912,7 +983,7 @@
         16,
     )
     vmem = pl.BlockSpec(memory_space=pltpu.VMEM)
-    chunks = padded_keys // LANES
+    chunks = (padded_keys - (n - 2) * tok_rows) // LANES
     result, decode_state = vmem_call(
         functools.partial(late_kernel, sizes),
         (
@@ -925,12 +996,13 @@
             step_queries,
             local_tail,
             local,
-            pair_planes(keys_values),
-            pair_planes(twin_pairs),
+            own_planes,
+            twin_planes,
             pair_planes(across_pairs),
             pair_planes(far_pairs),
             step_pairs,
             prior,
+            part,
         ),
         [
             pltpu.VMEM((TILE, LANES), bf16),
@@ -949,8 +1021,8 @@
     readout, decode_out = vmem_call(
         finish_kernel,
         (shape((heads * window_rows, LANES), bf16), shape((heads * step_rows, LANES), bf16)),
-        (result, got),
-        [pltpu.VMEM(got.shape, bf16), pltpu.SemaphoreType.DMA((2,))],
+        (result, got, got_tail),
+        [pltpu.VMEM(result.shape, bf16), pltpu.SemaphoreType.DMA((2,))],
         8,
         (hbm, hbm),
     )
@@ -977,7 +1049,7 @@
 
     def on_device(*arguments):
         n, rows_valid = lax.axis_size("ctx"), arguments[2].shape[1]
-        if n == 4 and rows_valid % 16 == 0:
+        if n == 4 and rows_valid % 16 == 0 and 2 * arguments[0].shape[0] % LANES == 0:
             return on_device_exchange(*arguments)
         return on_device_gather(*arguments)
 

time: 59.7 us -> 41.4 us (0.69)
  waiting for transfers between devices: 22.1 us -> 6.93 us
  Pallas kernels: 26.9 us -> 24.2 us
    ppermute x4 -> x5, waiting for transfers between devices: 20.9 us -> 4.93 us  [swap_across(): return lax.ppermute(value, 'ctx', [(i, (i + 2) % n) for i in range(n)])]
    pallas_call x6 -> x8, Pallas kernels: 24 us -> 21.3 us  [vmem_call(): pl.pallas_call(kernel, out_shape=out_shape, in_specs=[smem if operand.ndi...]
    ppermute x4, starting transfers between devices: 3.35 us -> 2.45 us  [swap_twin(): return lax.ppermute(value, 'ctx', [(i, i ^ 1) for i in range(n)])]
    ppermute x4, waiting for transfers between devices: 1.18 us -> 2.01 us  [swap_twin(): return lax.ppermute(value, 'ctx', [(i, i ^ 1) for i in range(n)])]
    ppermute x4 -> x5, starting transfers between devices: 4.35 us -> 4.81 us  [swap_across(): return lax.ppermute(value, 'ctx', [(i, (i + 2) % n) for i in range(n)])]
  transfers between devices with their start and end apart: 8 -> 9, of which waited for: 3 -> 3; matrix products, arithmetic and copies ran while one was open for 1% -> 1% of each run, Pallas kernels for 23% -> 56%
where the time goes in v3:
time: 41.4 us; the launch traced here: 41.2 us
  Pallas kernels  24.2 us (58%)
  starting transfers between devices  7.26 us (18%)
  waiting for transfers between devices  6.93 us (17%)
  between operations  1.61 us (4%)
  local copies, waits for them, and re-layouts  1.14 us (3%)
    pallas_call x8, Pallas kernels, vmem_call(): pl.pallas_call(kernel, out_shape=out_shape, in_specs=[smem if operand.ndi...  21.3 us
    ppermute x5, waiting for transfers between devices, swap_across(): return lax.ppermute(value, 'ctx', [(i, (i + 2) % n) for i in range(n)])  4.93 us
    ppermute x5, starting transfers between devices, swap_across(): return lax.ppermute(value, 'ctx', [(i, (i + 2) % n) for i in range(n)])  4.81 us
    pallas_call x1, Pallas kernels, pick_both(): pl.pallas_call(pick_both_kernel, out_shape=jax.ShapeDtypeStruct(shape, pa...  2.89 us
    ppermute x4, starting transfers between devices, swap_twin(): return lax.ppermute(value, 'ctx', [(i, i ^ 1) for i in range(n)])  2.45 us
    ppermute x4, waiting for transfers between devices, swap_twin(): return lax.ppermute(value, 'ctx', [(i, i ^ 1) for i in range(n)])  2.01 us
    unnamed x9, local copies, waits for them, and re-layouts  0.94 us
  transfers between devices with their start and end apart: 9, of which 3 were waited for; matrix products, arithmetic and copies ran while one was open for 1% of the time, Pallas kernels for 56%

profile of v3, /device:TPU:1, one launch (start us, length us, event | category | flops | bytes accessed | tf_op | source)
XLA Modules:
  0.0 41.2 jit_solution(2995652390417778627)
XLA Ops:
  0.6 0.1 collective-permute-start.2
  0.7 2.7 %collective-permute-start.6 = (bf16[192,2,5,128]{3,1,2,0:T(2,128)(2,1)}, bf16[192,2,5,128]{3,1,2,0:T(2,128)(2,1)S(1)}, u32[]{:S(2)}, u32[]{:S(2)}) collective-permute-start(bf16[192,2,5,128]{3,1,2,0:T(2,128)(2,1)} %param.7), channel_id=1, source_target_pairs={{0,8},{4,12},{8,0},{12,4},{1,9},{5,13},{9,1},{13,5},{2,10},{6,14},... | collective-permute-start | bytes 1474568 | tf_op jit(solution)/shard_map/ppermute | solution.py:906
  3.4 0.0 copy-start.3
  3.4 0.0 copy-start.2
  3.4 2.9 %pick_both.1.own = bf16[32,7,2,128]{3,2,1,0:T(2,128)(2,1)} custom-call(s32[32]{0:T(128)} %ids_ref.1, bf16[18992,5,2,128]{3,2,1,0:T(2,128)(2,1)} %bitcast.36, bf16[18992,2,2,128]{3,2,1,0:T(2,128)(2,1)} %pair_table.1), custom_call_target="tpu_custom_call" | custom-call | tf_op jit(solution)/shard_map/pick_both/pallas_call | solution.py:846
  6.3 0.0 copy-start
  6.3 0.5 %collective-permute-start = (bf16[32,7,2,128]{3,2,1,0:T(2,128)(2,1)}, bf16[32,7,2,128]{3,2,1,0:T(2,128)(2,1)S(1)}, u32[]{:S(2)}, u32[]{:S(2)}) collective-permute-start(bf16[32,7,2,128]{3,2,1,0:T(2,128)(2,1)} %pick_both.1.own), channel_id=1, source_target_pairs={{0,4},{4,0},{8,12},{12,8},{1,5},{5,1},{9,13},{13,9},{2,6},{6,2},{1... | collective-permute-start | bytes 344072 | tf_op jit(solution)/shard_map/ppermute | solution.py:909
  6.9 0.0 copy-done.3
  6.9 0.1 collective-permute-start.4
  7.0 1.1 %collective-permute-done.twin = bf16[32,7,2,128]{3,2,1,0:T(2,128)(2,1)S(1)} collective-permute-done((bf16[32,7,2,128]{3,2,1,0:T(2,128)(2,1)}, bf16[32,7,2,128]{3,2,1,0:T(2,128)(2,1)S(1)}, u32[]{:S(2)}, u32[]{:S(2)}) %collective-permute-start) | collective-permute-done | bytes 114720 | tf_op jit(solution)/shard_map/ppermute | solution.py:909
  8.0 0.0 copy-start.1
  8.0 0.9 %copy-done.1 = bf16[32,7,2,128]{3,2,1,0:T(2,128)(2,1)S(1)} copy-done((bf16[32,7,2,128]{3,2,1,0:T(2,128)(2,1)S(1)}, bf16[32,7,2,128]{3,2,1,0:T(2,128)(2,1)}, u32[]{:S(2)}) %copy-start.1) | copy-done | bytes 114712
  8.9 0.1 shard_map.94
  9.0 0.5 %collective-permute-start.1 = (bf16[144,2,128]{2,1,0:T(2,128)(2,1)S(1)}, bf16[144,2,128]{2,1,0:T(2,128)(2,1)S(1)}, u32[]{:S(2)}, u32[]{:S(2)}) collective-permute-start(bf16[144,2,128]{2,1,0:T(2,128)(2,1)S(1)} %shard_map.94), channel_id=1, source_target_pairs={{0,8},{4,12},{8,0},{12,4},{1,9},{5,13},{9,1},{13,5},{2,10},{6,14},... | collective-permute-start | bytes 221192 | tf_op jit(solution)/shard_map/ppermute | solution.py:906
  10.1 0.0 copy-done.2
  10.1 0.1 copy.24.queries
  10.2 4.9 %collective-permute-done.6 = bf16[192,2,5,128]{3,1,2,0:T(2,128)(2,1)S(1)} collective-permute-done((bf16[192,2,5,128]{3,1,2,0:T(2,128)(2,1)}, bf16[192,2,5,128]{3,1,2,0:T(2,128)(2,1)S(1)}, u32[]{:S(2)}, u32[]{:S(2)}) %collective-permute-start.6) | collective-permute-done | bytes 491552 | tf_op jit(solution)/shard_map/ppermute | solution.py:906
  15.1 0.1 copy.25.queries
  15.2 0.0 collective-permute-done.2.other
  15.2 0.0 copy-done
  15.2 5.0 %shard_map.95 = (bf16[2,128,4224]{2,1,0:T(8,128)(2,1)S(1)}, f32[2,768,128]{2,1,0:T(8,128)S(1)}) custom-call(bf16[2,960,128]{2,1,0:T(8,128)(2,1)S(1)} %copy.24.queries, bf16[2,2064,128]{2,1,0:T(8,128)(2,1)S(1)} %copy-done, bf16[2,2064,128]{2,1,0:T(8,128)(2,1)S(1)} %collective-permute-done.2.other), custom_call_target="tpu_custom_call" | custom-call | tf_op jit(solution)/shard_map/pallas_call | solution.py:864
  20.3 2.9 %shard_map.99 = bf16[1024,128]{1,0:T(8,128)(2,1)S(1)} custom-call(s32[1]{0:T(128)S(6)} %copy.38.counts, bf16[2,960,128]{2,1,0:T(8,128)(2,1)S(1)} %copy.25.queries, bf16[2,128,4224]{2,1,0:T(8,128)(2,1)S(1)} %get-tuple-element.9.turned), custom_call_target="tpu_custom_call" | custom-call | tf_op jit(solution)/shard_map/pallas_call | solution.py:864
  23.2 1.3 %collective-permute-start.7 = (bf16[1024,128]{1,0:T(8,128)(2,1)S(1)}, bf16[1024,128]{1,0:T(8,128)(2,1)S(1)}, u32[]{:S(2)}, u32[]{:S(2)}) collective-permute-start(bf16[1024,128]{1,0:T(8,128)(2,1)S(1)} %shard_map.99), channel_id=1, source_target_pairs={{0,8},{4,12},{8,0},{12,4},{1,9},{5,13},{9,1},{13,5},{2,10},{6,14},... | collective-permute-start | bytes 786440 | tf_op jit(solution)/shard_map/ppermute | solution.py:906
  24.5 0.0 collective-permute-done.1
  24.5 0.1 add.3
  24.6 3.7 %shard_map.100 = bf16[976,128]{1,0:T(8,128)(2,1)S(1)} custom-call(s32[1]{0:T(128)S(6)} %copy.38.counts, bf16[2,960,128]{2,1,0:T(8,128)(2,1)S(1)} %copy.25.queries, bf16[2,2,40,128]{3,2,1,0:T(8,128)(2,1)S(1)} %bitcast.30, bf16[2,128,4224]{2,1,0:T(8,128)(2,1)S(1)} %get-tuple-element.9.turned), custom_call_target="tpu_custom_call" | custom-call | tf_op jit(solution)/shard_map/pallas_call | solution.py:864
  28.3 0.3 collective-permute-start.8
  28.7 1.7 %collective-permute-start.3 = (bf16[192,2,2,128]{3,0,1,2:T(8,128)(2,1)S(1)}, bf16[192,2,2,128]{3,0,1,2:T(8,128)(2,1)S(1)}, u32[]{:S(2)}, u32[]{:S(2)}) collective-permute-start(bf16[192,2,2,128]{3,0,1,2:T(8,128)(2,1)S(1)} %copy.37), channel_id=1, source_target_pairs={{0,4},{4,0},{8,12},{12,8},{1,5},{5,1},{9,13},{13,9},{2,6},{6,2},{1... | collective-permute-start | bytes 589832 | tf_op jit(solution)/shard_map/ppermute | solution.py:909
  30.4 0.0 collective-permute-done.4
  30.4 0.1 collective-permute-start.5
  30.5 0.9 %collective-permute-done.3 = bf16[192,2,2,128]{3,0,1,2:T(8,128)(2,1)S(1)} collective-permute-done((bf16[192,2,2,128]{3,0,1,2:T(8,128)(2,1)S(1)}, bf16[192,2,2,128]{3,0,1,2:T(8,128)(2,1)S(1)}, u32[]{:S(2)}, u32[]{:S(2)}) %collective-permute-start.3) | collective-permute-done | bytes 196640 | tf_op jit(solution)/shard_map/ppermute | solution.py:909
  31.5 1.9 %shard_map.97.part = f32[2,2176,128]{2,1,0:T(8,128)S(1)} custom-call(bf16[2,2,192,128]{3,2,1,0:T(8,128)(2,1)S(1)} %bitcast.26, bf16[2,2,192,128]{3,2,1,0:T(8,128)(2,1)S(1)} %bitcast.28), custom_call_target="tpu_custom_call" | custom-call | tf_op jit(solution)/shard_map/pallas_call | solution.py:864
  33.4 1.7 %shard_map.96.local_tail = f32[2,256,128]{2,1,0:T(8,128)S(1)} custom-call(bf16[2,960,128]{2,1,0:T(8,128)(2,1)S(1)} %copy.24.queries, bf16[2,2,40,128]{3,2,1,0:T(8,128)(2,1)S(1)} %bitcast.31, bf16[2,128,4224]{2,1,0:T(8,128)(2,1)S(1)} %get-tuple-element.9.turned), custom_call_target="tpu_custom_call" | custom-call | tf_op jit(solution)/shard_map/pallas_call | solution.py:864
  35.0 0.0 collective-permute-done.5
  35.1 5.1 %shard_map.98 = (f32[2000,128]{1,0:T(8,128)S(1)}, f32[2,2064,128]{2,1,0:T(8,128)}) custom-call(s32[1]{0:T(128)S(6)} %copy.38.counts, bf16[2,960,128]{2,1,0:T(8,128)(2,1)S(1)} %copy.24.queries, bf16[2,2,40,128]{3,2,1,0:T(8,128)(2,1)S(1)} %bitcast.32, f32[2,256,128]{2,1,0:T(8,128)S(1)} %shard_map.96.local_tail, f32[2,768,128]{2,1,0:T(8,128)S(1)} %get-tuple-element.10.local, ...), custom_call_target="tpu_custom_call" | custom-call | tf_op jit(solution)/shard_map/pallas_call | solution.py:864
  40.1 0.0 collective-permute-done.8.got_tail
  40.1 0.0 collective-permute-done.7.got
  40.1 0.9 %shard_map.101 = (bf16[1920,128]{1,0:T(8,128)(2,1)}, bf16[80,128]{1,0:T(8,128)(2,1)}) custom-call(f32[2000,128]{1,0:T(8,128)S(1)} %get-tuple-element.11.result, bf16[1024,128]{1,0:T(8,128)(2,1)S(1)} %collective-permute-done.7.got, bf16[976,128]{1,0:T(8,128)(2,1)S(1)} %collective-permute-done.8.got_tail), custom_call_target="tpu_custom_call" | custom-call | tf_op jit(solution)/shard_map/pallas_call | solution.py:864
  (5 shorter events, 0.1 us)
Async XLA Ops:
  0.6 14.6 %collective-permute-start.2 = (bf16[2,2064,128]{2,1,0:T(8,128)(2,1)}, bf16[2,2064,128]{2,1,0:T(8,128)(2,1)S(1)}, u32[]{:S(2)}, u32[]{:S(2)}) collective-permute-start(bf16[2,2064,128]{2,1,0:T(8,128)(2,1)} %prior.1), channel_id=1, source_target_pairs={{0,4},{4,0},{8,12},{12,8},{1,5},{5,1},{9,13},{13,9},{2,6},{6,2},{1... | collective-permute-start | bytes 3170312 | tf_op jit(solution)/shard_map/ppermute | solution.py:909
  0.7 14.4 %collective-permute-start.6 = (bf16[192,2,5,128]{3,1,2,0:T(2,128)(2,1)}, bf16[192,2,5,128]{3,1,2,0:T(2,128)(2,1)S(1)}, u32[]{:S(2)}, u32[]{:S(2)}) collective-permute-start(bf16[192,2,5,128]{3,1,2,0:T(2,128)(2,1)} %param.7), channel_id=1, source_target_pairs={{0,8},{4,12},{8,0},{12,4},{1,9},{5,13},{9,1},{13,5},{2,10},{6,14},... | collective-permute-start | bytes 1474568 | tf_op jit(solution)/shard_map/ppermute | solution.py:906
  3.4 3.5 %copy-start.3 = (bf16[192,2,2,128]{3,2,1,0:T(2,128)(2,1)S(1)}, bf16[192,2,2,128]{3,2,1,0:T(2,128)(2,1)}, u32[]{:S(2)}) copy-start(bf16[192,2,2,128]{3,2,1,0:T(2,128)(2,1)} %param.8) | copy-start | bytes 589828
  3.4 6.7 %copy-start.2 = (bf16[192,2,5,128]{3,1,2,0:T(2,128)(2,1)S(1)}, bf16[192,2,5,128]{3,1,2,0:T(2,128)(2,1)}, u32[]{:S(2)}) copy-start(bf16[192,2,5,128]{3,1,2,0:T(2,128)(2,1)} %param.7) | copy-start | bytes 1474564
  6.3 8.9 %copy-start = (bf16[2,2064,128]{2,1,0:T(8,128)(2,1)S(1)}, bf16[2,2064,128]{2,1,0:T(8,128)(2,1)}, u32[]{:S(2)}) copy-start(bf16[2,2064,128]{2,1,0:T(8,128)(2,1)} %prior.1) | copy-start | bytes 3170308
  6.3 1.7 %collective-permute-start = (bf16[32,7,2,128]{3,2,1,0:T(2,128)(2,1)}, bf16[32,7,2,128]{3,2,1,0:T(2,128)(2,1)S(1)}, u32[]{:S(2)}, u32[]{:S(2)}) collective-permute-start(bf16[32,7,2,128]{3,2,1,0:T(2,128)(2,1)} %pick_both.1.own), channel_id=1, source_target_pairs={{0,4},{4,0},{8,12},{12,8},{1,5},{5,1},{9,13},{13,9},{2,6},{6,2},{1... | collective-permute-start | bytes 344072 | tf_op jit(solution)/shard_map/ppermute | solution.py:909
  6.9 23.5 %collective-permute-start.4 = (bf16[192,2,2,128]{3,0,1,2:T(8,128)(2,1)S(1)}, bf16[192,2,2,128]{3,0,1,2:T(8,128)(2,1)S(1)}, u32[]{:S(2)}, u32[]{:S(2)}) collective-permute-start(bf16[192,2,2,128]{3,0,1,2:T(8,128)(2,1)S(1)} %copy.37), channel_id=1, source_target_pairs={{0,8},{4,12},{8,0},{12,4},{1,9},{5,13},{9,1},{13,5},{2,10},{6,14},... | collective-permute-start | bytes 589832 | tf_op jit(solution)/shard_map/ppermute | solution.py:906
  8.0 0.9 %copy-start.1 = (bf16[32,7,2,128]{3,2,1,0:T(2,128)(2,1)S(1)}, bf16[32,7,2,128]{3,2,1,0:T(2,128)(2,1)}, u32[]{:S(2)}) copy-start(bf16[32,7,2,128]{3,2,1,0:T(2,128)(2,1)} %pick_both.1.own) | copy-start | bytes 344068
  9.0 15.5 %collective-permute-start.1 = (bf16[144,2,128]{2,1,0:T(2,128)(2,1)S(1)}, bf16[144,2,128]{2,1,0:T(2,128)(2,1)S(1)}, u32[]{:S(2)}, u32[]{:S(2)}) collective-permute-start(bf16[144,2,128]{2,1,0:T(2,128)(2,1)S(1)} %shard_map.94), channel_id=1, source_target_pairs={{0,8},{4,12},{8,0},{12,4},{1,9},{5,13},{9,1},{13,5},{2,10},{6,14},... | collective-permute-start | bytes 221192 | tf_op jit(solution)/shard_map/ppermute | solution.py:906
  23.2 16.9 %collective-permute-start.7 = (bf16[1024,128]{1,0:T(8,128)(2,1)S(1)}, bf16[1024,128]{1,0:T(8,128)(2,1)S(1)}, u32[]{:S(2)}, u32[]{:S(2)}) collective-permute-start(bf16[1024,128]{1,0:T(8,128)(2,1)S(1)} %shard_map.99), channel_id=1, source_target_pairs={{0,8},{4,12},{8,0},{12,4},{1,9},{5,13},{9,1},{13,5},{2,10},{6,14},... | collective-permute-start | bytes 786440 | tf_op jit(solution)/shard_map/ppermute | solution.py:906
  28.3 11.8 %collective-permute-start.8 = (bf16[976,128]{1,0:T(8,128)(2,1)S(1)}, bf16[976,128]{1,0:T(8,128)(2,1)S(1)}, u32[]{:S(2)}, u32[]{:S(2)}) collective-permute-start(bf16[976,128]{1,0:T(8,128)(2,1)S(1)} %shard_map.100), channel_id=1, source_target_pairs={{0,8},{4,12},{8,0},{12,4},{1,9},{5,13},{9,1},{13,5},{2,10},{6,14},... | collective-permute-start | bytes 749576 | tf_op jit(solution)/shard_map/ppermute | solution.py:906
  28.7 2.8 %collective-permute-start.3 = (bf16[192,2,2,128]{3,0,1,2:T(8,128)(2,1)S(1)}, bf16[192,2,2,128]{3,0,1,2:T(8,128)(2,1)S(1)}, u32[]{:S(2)}, u32[]{:S(2)}) collective-permute-start(bf16[192,2,2,128]{3,0,1,2:T(8,128)(2,1)S(1)} %copy.37), channel_id=1, source_target_pairs={{0,4},{4,0},{8,12},{12,8},{1,5},{5,1},{9,13},{13,9},{2,6},{6,2},{1... | collective-permute-start | bytes 589832 | tf_op jit(solution)/shard_map/ppermute | solution.py:909
  30.4 4.6 %collective-permute-start.5 = (bf16[192,2,2,128]{3,0,1,2:T(8,128)(2,1)S(1)}, bf16[192,2,2,128]{3,0,1,2:T(8,128)(2,1)S(1)}, u32[]{:S(2)}, u32[]{:S(2)}) collective-permute-start(bf16[192,2,2,128]{3,0,1,2:T(8,128)(2,1)S(1)} %collective-permute-done.4), channel_id=1, source_target_pairs={{0,4},{4,0},{8,12},{12,8},{1,5},{5,1},{9,13},{13,9},{2,6},{6,2},{1... | collective-permute-start | bytes 589832 | tf_op jit(solution)/shard_map/ppermute | solution.py:909

commit v4 on v3

--- a/solution.py
+++ b/solution.py
@@ -12,6 +12,7 @@
 MESH = pl.DeviceIdType.MESH
 TILE = 256
 LANES = 128
+PIECES = 4
 CONTRACT_LAST = (((1,), (1,)), ((), ()))
 
 
@@ -580,7 +581,7 @@
 
 def rows_scale(sizes, counts, position):
     token = jnp.floor((position.astype(jnp.float32) + 0.5) / sizes[2])
-    place_in_prompt = token + (counts[0] + 1).astype(jnp.float32)
+    place_in_prompt = token + counts[pl.ds(0, 1), pl.ds(0, 1)]
     return 1.0 / (LANES * jnp.sqrt(place_in_prompt))
 
 
@@ -657,18 +658,23 @@
 
 
 def finish_kernel(result, got, got_tail, window_out, step_out, total, sems):
-    rows = window_out.shape[0]
-    for part, first in ((got, 0), (got_tail, got.shape[0])):
-        at = pl.ds(first, part.shape[0])
-        total[at, :] = (result[at, :] + part[...].astype(jnp.float32)).astype(total.dtype)
-    copies = (
-        pltpu.make_async_copy(total.at[pl.ds(0, rows)], window_out, sems.at[0]),
-        pltpu.make_async_copy(
-            total.at[pl.ds(rows, total.shape[0] - rows)], step_out, sems.at[1]
-        ),
-    )
-    for copy in copies:
+    split = window_out.shape[0]
+    piece = round_up(total.shape[0], 16 * PIECES) // PIECES
+    cuts = sorted({*range(0, total.shape[0], piece), got.shape[0], split, total.shape[0]})
+    copies = []
+    for first, last in zip(cuts, cuts[1:]):
+        at = pl.ds(first, last - first)
+        part, base = (got, 0) if last <= got.shape[0] else (got_tail, got.shape[0])
+        rows = part[pl.ds(first - base, last - first), :].astype(jnp.float32)
+        total[at, :] = (result[at, :] + rows).astype(total.dtype)
+        target, base = (window_out, 0) if last <= split else (step_out, split)
+        copy = pltpu.make_async_copy(
+            total.at[at],
+            target.at[pl.ds(first - base, last - first)],
+            sems.at[len(copies)],
+        )
         copy.start()
+        copies.append(copy)
     for copy in copies:
         copy.wait()
 
@@ -818,7 +824,9 @@
         state_copy(head).wait()
 
 
-def pick_both_kernel(ids_ref, query_table, pair_table, picked, query_sem, pair_sem):
+def pick_both_kernel(
+    ids_ref, counts, query_table, pair_table, picked, origin, query_sem, pair_sem
+):
     vocab_rows, group = query_table.shape[:2]
     first_row = lax.axis_index("ctx") * vocab_rows
     heads = pair_table.shape[1]
@@ -838,33 +846,37 @@
         each(step, lambda copy: copy.start())
     for step in range(picked.shape[0]):
         each(step, lambda copy: copy.wait())
-
-
-def pick_both(ids, query_table, pair_table):
+    origin[...] = jnp.full(origin.shape, counts[0] + 1, jnp.int32).astype(jnp.float32)
+
+
+def pick_both(ids, counts, query_table, pair_table):
     steps, group, heads = ids.shape[0], query_table.shape[1], pair_table.shape[1]
     shape = (steps, group + heads) + pair_table.shape[2:]
     return pl.pallas_call(
         pick_both_kernel,
-        out_shape=jax.ShapeDtypeStruct(shape, pair_table.dtype),
+        out_shape=(pltpu.VMEM(shape, pair_table.dtype), pltpu.VMEM((8, LANES), jnp.float32)),
         in_specs=[
+            pl.BlockSpec(memory_space=pltpu.SMEM),
             pl.BlockSpec(memory_space=pltpu.SMEM),
             pl.BlockSpec(memory_space=pl.ANY),
             pl.BlockSpec(memory_space=pl.ANY),
         ],
-        out_specs=pl.BlockSpec(memory_space=pltpu.VMEM),
-        scratch_shapes=[pltpu.SemaphoreType.DMA((steps,)), pltpu.SemaphoreType.DMA((steps,))],
+        out_specs=(pl.BlockSpec(memory_space=pltpu.VMEM), pl.BlockSpec(memory_space=pltpu.VMEM)),
+        scratch_shapes=[
+            pltpu.SemaphoreType.DMA((steps,)),
+            pltpu.SemaphoreType.DMA((steps,)),
+        ],
         compiler_params=pltpu.CompilerParams(vmem_limit_bytes=56 * 2**20),
         name="pick_both",
-    )(ids, query_table, pair_table)
+    )(ids, counts, query_table, pair_table)
 
 
 def vmem_call(kernel, out_shape, operands, scratch, limit, out_specs=None):
-    smem = pl.BlockSpec(memory_space=pltpu.SMEM)
     vmem = pl.BlockSpec(memory_space=pltpu.VMEM)
     return pl.pallas_call(
         kernel,
         out_shape=out_shape,
-        in_specs=[smem if operand.ndim == 1 else vmem for operand in operands],
+        in_specs=[vmem] * len(operands),
         out_specs=out_specs if out_specs is not None else jax.tree.map(lambda _: vmem, out_shape),
         scratch_shapes=scratch,
         compiler_params=pltpu.CompilerParams(vmem_limit_bytes=limit * 2**20),
@@ -918,7 +930,7 @@
     across_pairs = swap_across(keys_values)
     twin_prior = swap_twin(prior)
     twin_pairs = swap_twin(keys_values)
-    picked = pick_both(continuation, query_table.transpose(0, 2, 1, 3), pair_table)
+    picked, counts = pick_both(continuation, counts, query_table.transpose(0, 2, 1, 3), pair_table)
     twin_picked = swap_twin(picked)
     send = vmem_call(
         functools.partial(merge_kernel, n),
@@ -1022,7 +1034,7 @@
         finish_kernel,
         (shape((heads * window_rows, LANES), bf16), shape((heads * step_rows, LANES), bf16)),
         (result, got, got_tail),
-        [pltpu.VMEM(result.shape, bf16), pltpu.SemaphoreType.DMA((2,))],
+        [pltpu.VMEM(result.shape, bf16), pltpu.SemaphoreType.DMA((PIECES + 3,))],
         8,
         (hbm, hbm),
     )

time: 41.4 us -> 42.1 us (1.017)
  waiting for transfers between devices: 6.93 us -> 8.27 us
  local copies, waits for them, and re-layouts: 1.14 us -> 0.25 us
    ppermute x5, waiting for transfers between devices: 4.93 us -> 6.47 us  [swap_across(): return lax.ppermute(value, 'ctx', [(i, (i + 2) % n) for i in range(n)])]
    unnamed x9 -> x7, local copies, waits for them, and re-layouts: 0.94 us -> 0.04 us
where the time goes in v4:
time: 42.1 us; the launch traced here: 41.9 us
  Pallas kernels  24.2 us (57%)
  waiting for transfers between devices  8.27 us (20%)
  starting transfers between devices  7.45 us (18%)
  between operations  1.61 us (4%)
    pallas_call x8, Pallas kernels, vmem_call(): pl.pallas_call(kernel, out_shape=out_shape, in_specs=[vmem] * len(operand...  22 us
    ppermute x5, waiting for transfers between devices, swap_across(): return lax.ppermute(value, 'ctx', [(i, (i + 2) % n) for i in range(n)])  6.47 us
    ppermute x5, starting transfers between devices, swap_across(): return lax.ppermute(value, 'ctx', [(i, (i + 2) % n) for i in range(n)])  5.2 us
    pallas_call x1, Pallas kernels, pick_both(): pl.pallas_call(pick_both_kernel, out_shape=(pltpu.VMEM(shape, pair_table....  2.25 us
    ppermute x4, starting transfers between devices, swap_twin(): return lax.ppermute(value, 'ctx', [(i, i ^ 1) for i in range(n)])  2.25 us
    ppermute x4, waiting for transfers between devices, swap_twin(): return lax.ppermute(value, 'ctx', [(i, i ^ 1) for i in range(n)])  1.8 us
  transfers between devices with their start and end apart: 9, of which 3 were waited for; matrix products, arithmetic and copies ran while one was open for 1% of the time, Pallas kernels for 56%

profile of v4, /device:TPU:1, one launch (start us, length us, event | category | flops | bytes accessed | tf_op | source)
XLA Modules:
  0.0 41.9 jit_solution(10798617699114742094)
XLA Ops:
  0.6 0.1 collective-permute-start.2
  0.7 2.7 %collective-permute-start.6 = (bf16[192,2,5,128]{3,1,2,0:T(2,128)(2,1)}, bf16[192,2,5,128]{3,1,2,0:T(2,128)(2,1)S(1)}, u32[]{:S(2)}, u32[]{:S(2)}) collective-permute-start(bf16[192,2,5,128]{3,1,2,0:T(2,128)(2,1)} %param.7), channel_id=1, source_target_pairs={{0,8},{4,12},{8,0},{12,4},{1,9},{5,13},{9,1},{13,5},{2,10},{6,14},... | collective-permute-start | bytes 1474568 | tf_op jit(solution)/shard_map/ppermute | solution.py:918
  4.1 0.0 copy-start.2
  4.1 0.0 copy-start.1
  4.1 2.2 %pick_both.1 = (bf16[32,7,2,128]{3,2,1,0:T(2,128)(2,1)S(1)}, f32[8,128]{1,0:T(8,128)S(1)}) custom-call(s32[32]{0:T(128)} %ids_ref.1, s32[1]{0:T(128)S(6)} %copy.38.counts, bf16[18992,5,2,128]{3,2,1,0:T(2,128)(2,1)} %bitcast.36, bf16[18992,2,2,128]{3,2,1,0:T(2,128)(2,1)} %pair_table.1), custom_call_target="tpu_custom_call" | custom-call | tf_op jit(solution)/shard_map/pick_both/pallas_call | solution.py:855
  6.3 0.0 copy-start
  6.3 0.5 %collective-permute-start = (bf16[32,7,2,128]{3,2,1,0:T(2,128)(2,1)S(1)}, bf16[32,7,2,128]{3,2,1,0:T(2,128)(2,1)S(1)}, u32[]{:S(2)}, u32[]{:S(2)}) collective-permute-start(bf16[32,7,2,128]{3,2,1,0:T(2,128)(2,1)S(1)} %get-tuple-element.12.own), channel_id=1, source_target_pairs={{0,4},{4,0},{8,12},{12,8},{1,5},{5,1},{9,13},{13,9},{2,6},{6,2},{1... | collective-permute-start | bytes 344072 | tf_op jit(solution)/shard_map/ppermute | solution.py:921
  6.9 0.0 copy-done.2
  6.9 0.1 collective-permute-start.4
  7.0 0.9 %collective-permute-done.twin = bf16[32,7,2,128]{3,2,1,0:T(2,128)(2,1)S(1)} collective-permute-done((bf16[32,7,2,128]{3,2,1,0:T(2,128)(2,1)S(1)}, bf16[32,7,2,128]{3,2,1,0:T(2,128)(2,1)S(1)}, u32[]{:S(2)}, u32[]{:S(2)}) %collective-permute-start) | collective-permute-done | bytes 114720 | tf_op jit(solution)/shard_map/ppermute | solution.py:921
  7.8 0.1 shard_map.94
  7.9 0.7 %collective-permute-start.1 = (bf16[144,2,128]{2,1,0:T(2,128)(2,1)S(1)}, bf16[144,2,128]{2,1,0:T(2,128)(2,1)S(1)}, u32[]{:S(2)}, u32[]{:S(2)}) collective-permute-start(bf16[144,2,128]{2,1,0:T(2,128)(2,1)S(1)} %shard_map.94), channel_id=1, source_target_pairs={{0,8},{4,12},{8,0},{12,4},{1,9},{5,13},{9,1},{13,5},{2,10},{6,14},... | collective-permute-start | bytes 221192 | tf_op jit(solution)/shard_map/ppermute | solution.py:918
  8.6 0.0 copy-done.1
  8.6 0.1 copy.24.queries
  8.7 6.5 %collective-permute-done.6 = bf16[192,2,5,128]{3,1,2,0:T(2,128)(2,1)S(1)} collective-permute-done((bf16[192,2,5,128]{3,1,2,0:T(2,128)(2,1)}, bf16[192,2,5,128]{3,1,2,0:T(2,128)(2,1)S(1)}, u32[]{:S(2)}, u32[]{:S(2)}) %collective-permute-start.6) | collective-permute-done | bytes 491552 | tf_op jit(solution)/shard_map/ppermute | solution.py:918
  15.1 0.1 copy.25.queries
  15.2 0.0 collective-permute-done.2.other
  15.2 0.0 copy-done
  15.2 5.1 %shard_map.95 = (bf16[2,128,4224]{2,1,0:T(8,128)(2,1)S(1)}, f32[2,768,128]{2,1,0:T(8,128)S(1)}) custom-call(bf16[2,960,128]{2,1,0:T(8,128)(2,1)S(1)} %copy.24.queries, bf16[2,2064,128]{2,1,0:T(8,128)(2,1)S(1)} %copy-done, bf16[2,2064,128]{2,1,0:T(8,128)(2,1)S(1)} %collective-permute-done.2.other), custom_call_target="tpu_custom_call" | custom-call | tf_op jit(solution)/shard_map/pallas_call | solution.py:876
  20.3 3.0 %shard_map.99 = bf16[1024,128]{1,0:T(8,128)(2,1)S(1)} custom-call(f32[8,128]{1,0:T(8,128)S(1)} %get-tuple-element.11.counts, bf16[2,960,128]{2,1,0:T(8,128)(2,1)S(1)} %copy.25.queries, bf16[2,128,4224]{2,1,0:T(8,128)(2,1)S(1)} %get-tuple-element.13.turned), custom_call_target="tpu_custom_call" | custom-call | tf_op jit(solution)/shard_map/pallas_call | solution.py:876
  23.3 1.2 %collective-permute-start.7 = (bf16[1024,128]{1,0:T(8,128)(2,1)S(1)}, bf16[1024,128]{1,0:T(8,128)(2,1)S(1)}, u32[]{:S(2)}, u32[]{:S(2)}) collective-permute-start(bf16[1024,128]{1,0:T(8,128)(2,1)S(1)} %shard_map.99), channel_id=1, source_target_pairs={{0,8},{4,12},{8,0},{12,4},{1,9},{5,13},{9,1},{13,5},{2,10},{6,14},... | collective-permute-start | bytes 786440 | tf_op jit(solution)/shard_map/ppermute | solution.py:918
  24.6 0.0 collective-permute-done.1
  24.6 0.1 add.3
  24.7 3.8 %shard_map.100 = bf16[976,128]{1,0:T(8,128)(2,1)S(1)} custom-call(f32[8,128]{1,0:T(8,128)S(1)} %get-tuple-element.11.counts, bf16[2,960,128]{2,1,0:T(8,128)(2,1)S(1)} %copy.25.queries, bf16[2,2,40,128]{3,2,1,0:T(8,128)(2,1)S(1)} %bitcast.30, bf16[2,128,4224]{2,1,0:T(8,128)(2,1)S(1)} %get-tuple-element.13.turned), custom_call_target="tpu_custom_call" | custom-call | tf_op jit(solution)/shard_map/pallas_call | solution.py:876
  28.5 0.5 %collective-permute-start.8 = (bf16[976,128]{1,0:T(8,128)(2,1)S(1)}, bf16[976,128]{1,0:T(8,128)(2,1)S(1)}, u32[]{:S(2)}, u32[]{:S(2)}) collective-permute-start(bf16[976,128]{1,0:T(8,128)(2,1)S(1)} %shard_map.100), channel_id=1, source_target_pairs={{0,8},{4,12},{8,0},{12,4},{1,9},{5,13},{9,1},{13,5},{2,10},{6,14},... | collective-permute-start | bytes 749576 | tf_op jit(solution)/shard_map/ppermute | solution.py:918
  29.0 1.5 %collective-permute-start.3 = (bf16[192,2,2,128]{3,0,1,2:T(8,128)(2,1)S(1)}, bf16[192,2,2,128]{3,0,1,2:T(8,128)(2,1)S(1)}, u32[]{:S(2)}, u32[]{:S(2)}) collective-permute-start(bf16[192,2,2,128]{3,0,1,2:T(8,128)(2,1)S(1)} %copy.37), channel_id=1, source_target_pairs={{0,4},{4,0},{8,12},{12,8},{1,5},{5,1},{9,13},{13,9},{2,6},{6,2},{1... | collective-permute-start | bytes 589832 | tf_op jit(solution)/shard_map/ppermute | solution.py:921
  30.6 0.0 collective-permute-done.4
  30.6 0.1 collective-permute-start.5
  30.7 0.9 %collective-permute-done.3 = bf16[192,2,2,128]{3,0,1,2:T(8,128)(2,1)S(1)} collective-permute-done((bf16[192,2,2,128]{3,0,1,2:T(8,128)(2,1)S(1)}, bf16[192,2,2,128]{3,0,1,2:T(8,128)(2,1)S(1)}, u32[]{:S(2)}, u32[]{:S(2)}) %collective-permute-start.3) | collective-permute-done | bytes 196640 | tf_op jit(solution)/shard_map/ppermute | solution.py:921
  31.6 1.9 %shard_map.97.part = f32[2,2176,128]{2,1,0:T(8,128)S(1)} custom-call(bf16[2,2,192,128]{3,2,1,0:T(8,128)(2,1)S(1)} %bitcast.26, bf16[2,2,192,128]{3,2,1,0:T(8,128)(2,1)S(1)} %bitcast.28), custom_call_target="tpu_custom_call" | custom-call | tf_op jit(solution)/shard_map/pallas_call | solution.py:876
  33.5 1.7 %shard_map.96.local_tail = f32[2,256,128]{2,1,0:T(8,128)S(1)} custom-call(bf16[2,960,128]{2,1,0:T(8,128)(2,1)S(1)} %copy.24.queries, bf16[2,2,40,128]{3,2,1,0:T(8,128)(2,1)S(1)} %bitcast.31, bf16[2,128,4224]{2,1,0:T(8,128)(2,1)S(1)} %get-tuple-element.13.turned), custom_call_target="tpu_custom_call" | custom-call | tf_op jit(solution)/shard_map/pallas_call | solution.py:876
  35.2 0.0 collective-permute-done.5
  35.2 5.7 %shard_map.98 = (f32[2000,128]{1,0:T(8,128)S(1)}, f32[2,2064,128]{2,1,0:T(8,128)}) custom-call(f32[8,128]{1,0:T(8,128)S(1)} %get-tuple-element.11.counts, bf16[2,960,128]{2,1,0:T(8,128)(2,1)S(1)} %copy.24.queries, bf16[2,2,40,128]{3,2,1,0:T(8,128)(2,1)S(1)} %bitcast.32, f32[2,256,128]{2,1,0:T(8,128)S(1)} %shard_map.96.local_tail, ...), custom_call_target="tpu_custom_call" | custom-call | tf_op jit(solution)/shard_map/pallas_call | solution.py:876
  40.9 0.0 collective-permute-done.8.got_tail
  40.9 0.0 collective-permute-done.7.got
  40.9 0.9 %shard_map.101 = (bf16[1920,128]{1,0:T(8,128)(2,1)}, bf16[80,128]{1,0:T(8,128)(2,1)}) custom-call(f32[2000,128]{1,0:T(8,128)S(1)} %get-tuple-element.15.result, bf16[1024,128]{1,0:T(8,128)(2,1)S(1)} %collective-permute-done.7.got, bf16[976,128]{1,0:T(8,128)(2,1)S(1)} %collective-permute-done.8.got_tail), custom_call_target="tpu_custom_call" | custom-call | tf_op jit(solution)/shard_map/pallas_call | solution.py:876
  (5 shorter events, 0.1 us)
Async XLA Ops:
  0.6 14.6 %collective-permute-start.2 = (bf16[2,2064,128]{2,1,0:T(8,128)(2,1)}, bf16[2,2064,128]{2,1,0:T(8,128)(2,1)S(1)}, u32[]{:S(2)}, u32[]{:S(2)}) collective-permute-start(bf16[2,2064,128]{2,1,0:T(8,128)(2,1)} %prior.1), channel_id=1, source_target_pairs={{0,4},{4,0},{8,12},{12,8},{1,5},{5,1},{9,13},{13,9},{2,6},{6,2},{1... | collective-permute-start | bytes 3170312 | tf_op jit(solution)/shard_map/ppermute | solution.py:921
  0.7 14.4 %collective-permute-start.6 = (bf16[192,2,5,128]{3,1,2,0:T(2,128)(2,1)}, bf16[192,2,5,128]{3,1,2,0:T(2,128)(2,1)S(1)}, u32[]{:S(2)}, u32[]{:S(2)}) collective-permute-start(bf16[192,2,5,128]{3,1,2,0:T(2,128)(2,1)} %param.7), channel_id=1, source_target_pairs={{0,8},{4,12},{8,0},{12,4},{1,9},{5,13},{9,1},{13,5},{2,10},{6,14},... | collective-permute-start | bytes 1474568 | tf_op jit(solution)/shard_map/ppermute | solution.py:918
  4.1 2.8 %copy-start.2 = (bf16[192,2,2,128]{3,2,1,0:T(2,128)(2,1)S(1)}, bf16[192,2,2,128]{3,2,1,0:T(2,128)(2,1)}, u32[]{:S(2)}) copy-start(bf16[192,2,2,128]{3,2,1,0:T(2,128)(2,1)} %param.8) | copy-start | bytes 589828
  4.1 4.5 %copy-start.1 = (bf16[192,2,5,128]{3,1,2,0:T(2,128)(2,1)S(1)}, bf16[192,2,5,128]{3,1,2,0:T(2,128)(2,1)}, u32[]{:S(2)}) copy-start(bf16[192,2,5,128]{3,1,2,0:T(2,128)(2,1)} %param.7) | copy-start | bytes 1474564
  6.3 8.9 %copy-start = (bf16[2,2064,128]{2,1,0:T(8,128)(2,1)S(1)}, bf16[2,2064,128]{2,1,0:T(8,128)(2,1)}, u32[]{:S(2)}) copy-start(bf16[2,2064,128]{2,1,0:T(8,128)(2,1)} %prior.1) | copy-start | bytes 3170308
  6.3 1.5 %collective-permute-start = (bf16[32,7,2,128]{3,2,1,0:T(2,128)(2,1)S(1)}, bf16[32,7,2,128]{3,2,1,0:T(2,128)(2,1)S(1)}, u32[]{:S(2)}, u32[]{:S(2)}) collective-permute-start(bf16[32,7,2,128]{3,2,1,0:T(2,128)(2,1)S(1)} %get-tuple-element.12.own), channel_id=1, source_target_pairs={{0,4},{4,0},{8,12},{12,8},{1,5},{5,1},{9,13},{13,9},{2,6},{6,2},{1... | collective-permute-start | bytes 344072 | tf_op jit(solution)/shard_map/ppermute | solution.py:921
  6.9 23.7 %collective-permute-start.4 = (bf16[192,2,2,128]{3,0,1,2:T(8,128)(2,1)S(1)}, bf16[192,2,2,128]{3,0,1,2:T(8,128)(2,1)S(1)}, u32[]{:S(2)}, u32[]{:S(2)}) collective-permute-start(bf16[192,2,2,128]{3,0,1,2:T(8,128)(2,1)S(1)} %copy.37), channel_id=1, source_target_pairs={{0,8},{4,12},{8,0},{12,4},{1,9},{5,13},{9,1},{13,5},{2,10},{6,14},... | collective-permute-start | bytes 589832 | tf_op jit(solution)/shard_map/ppermute | solution.py:918
  7.9 16.6 %collective-permute-start.1 = (bf16[144,2,128]{2,1,0:T(2,128)(2,1)S(1)}, bf16[144,2,128]{2,1,0:T(2,128)(2,1)S(1)}, u32[]{:S(2)}, u32[]{:S(2)}) collective-permute-start(bf16[144,2,128]{2,1,0:T(2,128)(2,1)S(1)} %shard_map.94), channel_id=1, source_target_pairs={{0,8},{4,12},{8,0},{12,4},{1,9},{5,13},{9,1},{13,5},{2,10},{6,14},... | collective-permute-start | bytes 221192 | tf_op jit(solution)/shard_map/ppermute | solution.py:918
  23.3 17.6 %collective-permute-start.7 = (bf16[1024,128]{1,0:T(8,128)(2,1)S(1)}, bf16[1024,128]{1,0:T(8,128)(2,1)S(1)}, u32[]{:S(2)}, u32[]{:S(2)}) collective-permute-start(bf16[1024,128]{1,0:T(8,128)(2,1)S(1)} %shard_map.99), channel_id=1, source_target_pairs={{0,8},{4,12},{8,0},{12,4},{1,9},{5,13},{9,1},{13,5},{2,10},{6,14},... | collective-permute-start | bytes 786440 | tf_op jit(solution)/shard_map/ppermute | solution.py:918
  28.5 12.4 %collective-permute-start.8 = (bf16[976,128]{1,0:T(8,128)(2,1)S(1)}, bf16[976,128]{1,0:T(8,128)(2,1)S(1)}, u32[]{:S(2)}, u32[]{:S(2)}) collective-permute-start(bf16[976,128]{1,0:T(8,128)(2,1)S(1)} %shard_map.100), channel_id=1, source_target_pairs={{0,8},{4,12},{8,0},{12,4},{1,9},{5,13},{9,1},{13,5},{2,10},{6,14},... | collective-permute-start | bytes 749576 | tf_op jit(solution)/shard_map/ppermute | solution.py:918
  29.0 2.6 %collective-permute-start.3 = (bf16[192,2,2,128]{3,0,1,2:T(8,128)(2,1)S(1)}, bf16[192,2,2,128]{3,0,1,2:T(8,128)(2,1)S(1)}, u32[]{:S(2)}, u32[]{:S(2)}) collective-permute-start(bf16[192,2,2,128]{3,0,1,2:T(8,128)(2,1)S(1)} %copy.37), channel_id=1, source_target_pairs={{0,4},{4,0},{8,12},{12,8},{1,5},{5,1},{9,13},{13,9},{2,6},{6,2},{1... | collective-permute-start | bytes 589832 | tf_op jit(solution)/shard_map/ppermute | solution.py:921
  30.6 4.6 %collective-permute-start.5 = (bf16[192,2,2,128]{3,0,1,2:T(8,128)(2,1)S(1)}, bf16[192,2,2,128]{3,0,1,2:T(8,128)(2,1)S(1)}, u32[]{:S(2)}, u32[]{:S(2)}) collective-permute-start(bf16[192,2,2,128]{3,0,1,2:T(8,128)(2,1)S(1)} %collective-permute-done.4), channel_id=1, source_target_pairs={{0,4},{4,0},{8,12},{12,8},{1,5},{5,1},{9,13},{13,9},{2,6},{6,2},{1... | collective-permute-start | bytes 589832 | tf_op jit(solution)/shard_map/ppermute | solution.py:921

commit v5 on v4

--- a/solution.py
+++ b/solution.py
@@ -657,26 +657,34 @@
         local[head] = carry_tile(turned.at[head], first_offset, plain, scaled, 0)
 
 
-def finish_kernel(result, got, got_tail, window_out, step_out, total, sems):
+def add_out(result, got, first, window_out, step_out, total, sems):
     split = window_out.shape[0]
-    piece = round_up(total.shape[0], 16 * PIECES) // PIECES
-    cuts = sorted({*range(0, total.shape[0], piece), got.shape[0], split, total.shape[0]})
+    stop = first + got.shape[0]
+    piece = round_up(got.shape[0], 16 * PIECES) // PIECES
+    cuts = sorted({*range(first, stop, piece), min(max(split, first), stop), stop})
     copies = []
-    for first, last in zip(cuts, cuts[1:]):
-        at = pl.ds(first, last - first)
-        part, base = (got, 0) if last <= got.shape[0] else (got_tail, got.shape[0])
-        rows = part[pl.ds(first - base, last - first), :].astype(jnp.float32)
-        total[at, :] = (result[at, :] + rows).astype(total.dtype)
+    for start, last in zip(cuts, cuts[1:]):
+        at = pl.ds(start - first, last - start)
+        rows = result[pl.ds(start, last - start), :] + got[at, :].astype(jnp.float32)
+        total[at, :] = rows.astype(total.dtype)
         target, base = (window_out, 0) if last <= split else (step_out, split)
         copy = pltpu.make_async_copy(
             total.at[at],
-            target.at[pl.ds(first - base, last - first)],
+            target.at[pl.ds(start - base, last - start)],
             sems.at[len(copies)],
         )
         copy.start()
         copies.append(copy)
     for copy in copies:
         copy.wait()
+
+
+def finish_kernel(result, got, window_out, total, sems):
+    add_out(result, got, 0, window_out, None, total, sems)
+
+
+def finish_tail_kernel(first, result, got, window_in, window_out, step_out, total, sems):
+    add_out(result, got, first, window_out, step_out, total, sems)
 
 
 def state_blocks(load_keys, chunks, values, delta, keys_plain, keys_scaled, my_offset):
@@ -1030,14 +1038,29 @@
         (vmem, pl.BlockSpec(memory_space=pl.ANY)),
     )
     hbm = pl.BlockSpec(memory_space=pl.ANY)
-    readout, decode_out = vmem_call(
+    vmem = pl.BlockSpec(memory_space=pltpu.VMEM)
+    window_shape = shape((heads * window_rows, LANES), bf16)
+    sems = pltpu.SemaphoreType.DMA((PIECES + 2,))
+    params = pltpu.CompilerParams(vmem_limit_bytes=8 * 2**20)
+    readout = pl.pallas_call(
         finish_kernel,
-        (shape((heads * window_rows, LANES), bf16), shape((heads * step_rows, LANES), bf16)),
-        (result, got, got_tail),
-        [pltpu.VMEM(result.shape, bf16), pltpu.SemaphoreType.DMA((PIECES + 3,))],
-        8,
-        (hbm, hbm),
-    )
+        out_shape=window_shape,
+        in_specs=[vmem, vmem],
+        out_specs=hbm,
+        scratch_shapes=[pltpu.VMEM(got.shape, bf16), sems],
+        compiler_params=params,
+        name="finish",
+    )(result, got)
+    readout, decode_out = pl.pallas_call(
+        functools.partial(finish_tail_kernel, got.shape[0]),
+        out_shape=(window_shape, shape((heads * step_rows, LANES), bf16)),
+        in_specs=[vmem, vmem, hbm],
+        out_specs=(hbm, hbm),
+        scratch_shapes=[pltpu.VMEM(got_tail.shape, bf16), sems],
+        input_output_aliases={2: 0},
+        compiler_params=params,
+        name="finishtail",
+    )(result, got_tail, readout)
     readout = readout.reshape(tok_rows, group, heads, head_size)
     decode_out = decode_out.reshape(per_shard, group, heads, head_size)
     return (readout.transpose(0, 2, 1, 3), decode_out.transpose(0, 2, 1, 3), decode_state)

time: 42.1 us -> 42.8 us (1.017)
  Pallas kernels: 24.2 us -> 24.9 us
    pallas_call x0 -> x2, Pallas kernels: none -> 1.51 us  [the longest x1 0.76 us: on_device_exchange(): pl.pallas_call(finish_kernel, out_shape=window_shape, in_specs=[vmem, vme...]
    pallas_call x8 -> x7, Pallas kernels: 22 us -> 21.1 us  [vmem_call(): pl.pallas_call(kernel, out_shape=out_shape, in_specs=[vmem] * len(operand...]
  transfers between devices with their start and end apart: 9 -> 9, of which waited for: 3 -> 3; matrix products, arithmetic and copies ran while one was open for 1% -> 1% of each run, Pallas kernels for 56% -> 57%
where the time goes in v5:
time: 42.8 us; the launch traced here: 42.6 us
  Pallas kernels  24.9 us (58%)
  waiting for transfers between devices  8.27 us (19%)
  starting transfers between devices  7.45 us (17%)
  between operations  1.61 us (4%)
    pallas_call x7, Pallas kernels, vmem_call(): pl.pallas_call(kernel, out_shape=out_shape, in_specs=[vmem] * len(operand...  21.1 us
    ppermute x5, waiting for transfers between devices, swap_across(): return lax.ppermute(value, 'ctx', [(i, (i + 2) % n) for i in range(n)])  6.47 us
    ppermute x5, starting transfers between devices, swap_across(): return lax.ppermute(value, 'ctx', [(i, (i + 2) % n) for i in range(n)])  5.2 us
    pallas_call x1, Pallas kernels, pick_both(): pl.pallas_call(pick_both_kernel, out_shape=(pltpu.VMEM(shape, pair_table....  2.25 us
    ppermute x4, starting transfers between devices, swap_twin(): return lax.ppermute(value, 'ctx', [(i, i ^ 1) for i in range(n)])  2.25 us
    ppermute x4, waiting for transfers between devices, swap_twin(): return lax.ppermute(value, 'ctx', [(i, i ^ 1) for i in range(n)])  1.8 us
  transfers between devices with their start and end apart: 9, of which 3 were waited for; matrix products, arithmetic and copies ran while one was open for 1% of the time, Pallas kernels for 57%

profile of v5, /device:TPU:1, one launch (start us, length us, event | category | flops | bytes accessed | tf_op | source)
XLA Modules:
  0.0 42.6 jit_solution(15407216739137626207)
XLA Ops:
  0.6 0.1 collective-permute-start.2
  0.7 2.7 %collective-permute-start.6 = (bf16[192,2,5,128]{3,1,2,0:T(2,128)(2,1)}, bf16[192,2,5,128]{3,1,2,0:T(2,128)(2,1)S(1)}, u32[]{:S(2)}, u32[]{:S(2)}) collective-permute-start(bf16[192,2,5,128]{3,1,2,0:T(2,128)(2,1)} %param.7), channel_id=1, source_target_pairs={{0,8},{4,12},{8,0},{12,4},{1,9},{5,13},{9,1},{13,5},{2,10},{6,14},... | collective-permute-start | bytes 1474568 | tf_op jit(solution)/shard_map/ppermute | solution.py:926
  4.1 0.0 copy-start.2
  4.1 0.0 copy-start.1
  4.1 2.2 %pick_both.1 = (bf16[32,7,2,128]{3,2,1,0:T(2,128)(2,1)S(1)}, f32[8,128]{1,0:T(8,128)S(1)}) custom-call(s32[32]{0:T(128)} %ids_ref.1, s32[1]{0:T(128)S(6)} %copy.40.counts, bf16[18992,5,2,128]{3,2,1,0:T(2,128)(2,1)} %bitcast.36, bf16[18992,2,2,128]{3,2,1,0:T(2,128)(2,1)} %pair_table.1), custom_call_target="tpu_custom_call" | custom-call | tf_op jit(solution)/shard_map/pick_both/pallas_call | solution.py:863
  6.3 0.0 copy-start
  6.3 0.5 %collective-permute-start = (bf16[32,7,2,128]{3,2,1,0:T(2,128)(2,1)S(1)}, bf16[32,7,2,128]{3,2,1,0:T(2,128)(2,1)S(1)}, u32[]{:S(2)}, u32[]{:S(2)}) collective-permute-start(bf16[32,7,2,128]{3,2,1,0:T(2,128)(2,1)S(1)} %get-tuple-element.12.own), channel_id=1, source_target_pairs={{0,4},{4,0},{8,12},{12,8},{1,5},{5,1},{9,13},{13,9},{2,6},{6,2},{1... | collective-permute-start | bytes 344072 | tf_op jit(solution)/shard_map/ppermute | solution.py:929
  6.9 0.0 copy-done.2
  6.9 0.1 collective-permute-start.4
  7.0 0.9 %collective-permute-done.twin = bf16[32,7,2,128]{3,2,1,0:T(2,128)(2,1)S(1)} collective-permute-done((bf16[32,7,2,128]{3,2,1,0:T(2,128)(2,1)S(1)}, bf16[32,7,2,128]{3,2,1,0:T(2,128)(2,1)S(1)}, u32[]{:S(2)}, u32[]{:S(2)}) %collective-permute-start) | collective-permute-done | bytes 114720 | tf_op jit(solution)/shard_map/ppermute | solution.py:929
  7.8 0.1 shard_map.94
  7.9 0.7 %collective-permute-start.1 = (bf16[144,2,128]{2,1,0:T(2,128)(2,1)S(1)}, bf16[144,2,128]{2,1,0:T(2,128)(2,1)S(1)}, u32[]{:S(2)}, u32[]{:S(2)}) collective-permute-start(bf16[144,2,128]{2,1,0:T(2,128)(2,1)S(1)} %shard_map.94), channel_id=1, source_target_pairs={{0,8},{4,12},{8,0},{12,4},{1,9},{5,13},{9,1},{13,5},{2,10},{6,14},... | collective-permute-start | bytes 221192 | tf_op jit(solution)/shard_map/ppermute | solution.py:926
  8.6 0.0 copy-done.1
  8.6 0.1 copy.25.queries
  8.7 6.5 %collective-permute-done.6 = bf16[192,2,5,128]{3,1,2,0:T(2,128)(2,1)S(1)} collective-permute-done((bf16[192,2,5,128]{3,1,2,0:T(2,128)(2,1)}, bf16[192,2,5,128]{3,1,2,0:T(2,128)(2,1)S(1)}, u32[]{:S(2)}, u32[]{:S(2)}) %collective-permute-start.6) | collective-permute-done | bytes 491552 | tf_op jit(solution)/shard_map/ppermute | solution.py:926
  15.1 0.1 copy.26.queries
  15.2 0.0 collective-permute-done.2.other
  15.2 0.0 copy-done
  15.2 5.1 %shard_map.95 = (bf16[2,128,4224]{2,1,0:T(8,128)(2,1)S(1)}, f32[2,768,128]{2,1,0:T(8,128)S(1)}) custom-call(bf16[2,960,128]{2,1,0:T(8,128)(2,1)S(1)} %copy.25.queries, bf16[2,2064,128]{2,1,0:T(8,128)(2,1)S(1)} %copy-done, bf16[2,2064,128]{2,1,0:T(8,128)(2,1)S(1)} %collective-permute-done.2.other), custom_call_target="tpu_custom_call" | custom-call | tf_op jit(solution)/shard_map/pallas_call | solution.py:884
  20.3 3.0 %shard_map.100 = bf16[1024,128]{1,0:T(8,128)(2,1)S(1)} custom-call(f32[8,128]{1,0:T(8,128)S(1)} %get-tuple-element.11.counts, bf16[2,960,128]{2,1,0:T(8,128)(2,1)S(1)} %copy.26.queries, bf16[2,128,4224]{2,1,0:T(8,128)(2,1)S(1)} %get-tuple-element.13.turned), custom_call_target="tpu_custom_call" | custom-call | tf_op jit(solution)/shard_map/pallas_call | solution.py:884
  23.3 1.2 %collective-permute-start.8 = (bf16[1024,128]{1,0:T(8,128)(2,1)S(1)}, bf16[1024,128]{1,0:T(8,128)(2,1)S(1)}, u32[]{:S(2)}, u32[]{:S(2)}) collective-permute-start(bf16[1024,128]{1,0:T(8,128)(2,1)S(1)} %shard_map.100), channel_id=1, source_target_pairs={{0,8},{4,12},{8,0},{12,4},{1,9},{5,13},{9,1},{13,5},{2,10},{6,14},... | collective-permute-start | bytes 786440 | tf_op jit(solution)/shard_map/ppermute | solution.py:926
  24.6 0.0 collective-permute-done.1
  24.6 0.1 add.3
  24.7 3.8 %shard_map.99 = bf16[976,128]{1,0:T(8,128)(2,1)S(1)} custom-call(f32[8,128]{1,0:T(8,128)S(1)} %get-tuple-element.11.counts, bf16[2,960,128]{2,1,0:T(8,128)(2,1)S(1)} %copy.26.queries, bf16[2,2,40,128]{3,2,1,0:T(8,128)(2,1)S(1)} %bitcast.30, bf16[2,128,4224]{2,1,0:T(8,128)(2,1)S(1)} %get-tuple-element.13.turned), custom_call_target="tpu_custom_call" | custom-call | tf_op jit(solution)/shard_map/pallas_call | solution.py:884
  28.5 0.5 %collective-permute-start.7 = (bf16[976,128]{1,0:T(8,128)(2,1)S(1)}, bf16[976,128]{1,0:T(8,128)(2,1)S(1)}, u32[]{:S(2)}, u32[]{:S(2)}) collective-permute-start(bf16[976,128]{1,0:T(8,128)(2,1)S(1)} %shard_map.99), channel_id=1, source_target_pairs={{0,8},{4,12},{8,0},{12,4},{1,9},{5,13},{9,1},{13,5},{2,10},{6,14},... | collective-permute-start | bytes 749576 | tf_op jit(solution)/shard_map/ppermute | solution.py:926
  29.0 1.5 %collective-permute-start.3 = (bf16[192,2,2,128]{3,0,1,2:T(8,128)(2,1)S(1)}, bf16[192,2,2,128]{3,0,1,2:T(8,128)(2,1)S(1)}, u32[]{:S(2)}, u32[]{:S(2)}) collective-permute-start(bf16[192,2,2,128]{3,0,1,2:T(8,128)(2,1)S(1)} %copy.38), channel_id=1, source_target_pairs={{0,4},{4,0},{8,12},{12,8},{1,5},{5,1},{9,13},{13,9},{2,6},{6,2},{1... | collective-permute-start | bytes 589832 | tf_op jit(solution)/shard_map/ppermute | solution.py:929
  30.6 0.0 collective-permute-done.4
  30.6 0.1 collective-permute-start.5
  30.7 0.9 %collective-permute-done.3 = bf16[192,2,2,128]{3,0,1,2:T(8,128)(2,1)S(1)} collective-permute-done((bf16[192,2,2,128]{3,0,1,2:T(8,128)(2,1)S(1)}, bf16[192,2,2,128]{3,0,1,2:T(8,128)(2,1)S(1)}, u32[]{:S(2)}, u32[]{:S(2)}) %collective-permute-start.3) | collective-permute-done | bytes 196640 | tf_op jit(solution)/shard_map/ppermute | solution.py:929
  31.6 1.9 %shard_map.97.part = f32[2,2176,128]{2,1,0:T(8,128)S(1)} custom-call(bf16[2,2,192,128]{3,2,1,0:T(8,128)(2,1)S(1)} %bitcast.26, bf16[2,2,192,128]{3,2,1,0:T(8,128)(2,1)S(1)} %bitcast.28), custom_call_target="tpu_custom_call" | custom-call | tf_op jit(solution)/shard_map/pallas_call | solution.py:884
  33.5 1.7 %shard_map.96.local_tail = f32[2,256,128]{2,1,0:T(8,128)S(1)} custom-call(bf16[2,960,128]{2,1,0:T(8,128)(2,1)S(1)} %copy.25.queries, bf16[2,2,40,128]{3,2,1,0:T(8,128)(2,1)S(1)} %bitcast.31, bf16[2,128,4224]{2,1,0:T(8,128)(2,1)S(1)} %get-tuple-element.13.turned), custom_call_target="tpu_custom_call" | custom-call | tf_op jit(solution)/shard_map/pallas_call | solution.py:884
  35.2 0.0 collective-permute-done.5
  35.2 5.7 %shard_map.98 = (f32[2000,128]{1,0:T(8,128)S(1)}, f32[2,2064,128]{2,1,0:T(8,128)}) custom-call(f32[8,128]{1,0:T(8,128)S(1)} %get-tuple-element.11.counts, bf16[2,960,128]{2,1,0:T(8,128)(2,1)S(1)} %copy.25.queries, bf16[2,2,40,128]{3,2,1,0:T(8,128)(2,1)S(1)} %bitcast.32, f32[2,256,128]{2,1,0:T(8,128)S(1)} %shard_map.96.local_tail, ...), custom_call_target="tpu_custom_call" | custom-call | tf_op jit(solution)/shard_map/pallas_call | solution.py:884
  40.9 0.0 collective-permute-done.8.got
  40.9 0.8 %finish.1.window_in = bf16[1920,128]{1,0:T(8,128)(2,1)} custom-call(f32[2000,128]{1,0:T(8,128)S(1)} %get-tuple-element.15.result, bf16[1024,128]{1,0:T(8,128)(2,1)S(1)} %collective-permute-done.8.got), custom_call_target="tpu_custom_call" | custom-call | tf_op jit(solution)/shard_map/finish/pallas_call | solution.py:1045
  41.6 0.0 collective-permute-done.7.got
  41.6 0.8 %finishtail.1 = (bf16[1920,128]{1,0:T(8,128)(2,1)}, bf16[80,128]{1,0:T(8,128)(2,1)}) custom-call(f32[2000,128]{1,0:T(8,128)S(1)} %get-tuple-element.15.result, bf16[976,128]{1,0:T(8,128)(2,1)S(1)} %collective-permute-done.7.got, bf16[1920,128]{1,0:T(8,128)(2,1)} %finish.1.window_in), custom_call_target="tpu_custom_call", output_to_operand_aliasing={{0}: (2, {})} | custom-call | tf_op jit(solution)/shard_map/finishtail/pallas_call | solution.py:1054
  (5 shorter events, 0.1 us)
Async XLA Ops:
  0.6 14.6 %collective-permute-start.2 = (bf16[2,2064,128]{2,1,0:T(8,128)(2,1)}, bf16[2,2064,128]{2,1,0:T(8,128)(2,1)S(1)}, u32[]{:S(2)}, u32[]{:S(2)}) collective-permute-start(bf16[2,2064,128]{2,1,0:T(8,128)(2,1)} %prior.1), channel_id=1, source_target_pairs={{0,4},{4,0},{8,12},{12,8},{1,5},{5,1},{9,13},{13,9},{2,6},{6,2},{1... | collective-permute-start | bytes 3170312 | tf_op jit(solution)/shard_map/ppermute | solution.py:929
  0.7 14.4 %collective-permute-start.6 = (bf16[192,2,5,128]{3,1,2,0:T(2,128)(2,1)}, bf16[192,2,5,128]{3,1,2,0:T(2,128)(2,1)S(1)}, u32[]{:S(2)}, u32[]{:S(2)}) collective-permute-start(bf16[192,2,5,128]{3,1,2,0:T(2,128)(2,1)} %param.7), channel_id=1, source_target_pairs={{0,8},{4,12},{8,0},{12,4},{1,9},{5,13},{9,1},{13,5},{2,10},{6,14},... | collective-permute-start | bytes 1474568 | tf_op jit(solution)/shard_map/ppermute | solution.py:926
  4.1 2.8 %copy-start.2 = (bf16[192,2,2,128]{3,2,1,0:T(2,128)(2,1)S(1)}, bf16[192,2,2,128]{3,2,1,0:T(2,128)(2,1)}, u32[]{:S(2)}) copy-start(bf16[192,2,2,128]{3,2,1,0:T(2,128)(2,1)} %param.8) | copy-start | bytes 589828
  4.1 4.5 %copy-start.1 = (bf16[192,2,5,128]{3,1,2,0:T(2,128)(2,1)S(1)}, bf16[192,2,5,128]{3,1,2,0:T(2,128)(2,1)}, u32[]{:S(2)}) copy-start(bf16[192,2,5,128]{3,1,2,0:T(2,128)(2,1)} %param.7) | copy-start | bytes 1474564
  6.3 8.9 %copy-start = (bf16[2,2064,128]{2,1,0:T(8,128)(2,1)S(1)}, bf16[2,2064,128]{2,1,0:T(8,128)(2,1)}, u32[]{:S(2)}) copy-start(bf16[2,2064,128]{2,1,0:T(8,128)(2,1)} %prior.1) | copy-start | bytes 3170308
  6.3 1.5 %collective-permute-start = (bf16[32,7,2,128]{3,2,1,0:T(2,128)(2,1)S(1)}, bf16[32,7,2,128]{3,2,1,0:T(2,128)(2,1)S(1)}, u32[]{:S(2)}, u32[]{:S(2)}) collective-permute-start(bf16[32,7,2,128]{3,2,1,0:T(2,128)(2,1)S(1)} %get-tuple-element.12.own), channel_id=1, source_target_pairs={{0,4},{4,0},{8,12},{12,8},{1,5},{5,1},{9,13},{13,9},{2,6},{6,2},{1... | collective-permute-start | bytes 344072 | tf_op jit(solution)/shard_map/ppermute | solution.py:929
  6.9 23.7 %collective-permute-start.4 = (bf16[192,2,2,128]{3,0,1,2:T(8,128)(2,1)S(1)}, bf16[192,2,2,128]{3,0,1,2:T(8,128)(2,1)S(1)}, u32[]{:S(2)}, u32[]{:S(2)}) collective-permute-start(bf16[192,2,2,128]{3,0,1,2:T(8,128)(2,1)S(1)} %copy.38), channel_id=1, source_target_pairs={{0,8},{4,12},{8,0},{12,4},{1,9},{5,13},{9,1},{13,5},{2,10},{6,14},... | collective-permute-start | bytes 589832 | tf_op jit(solution)/shard_map/ppermute | solution.py:926
  7.9 16.6 %collective-permute-start.1 = (bf16[144,2,128]{2,1,0:T(2,128)(2,1)S(1)}, bf16[144,2,128]{2,1,0:T(2,128)(2,1)S(1)}, u32[]{:S(2)}, u32[]{:S(2)}) collective-permute-start(bf16[144,2,128]{2,1,0:T(2,128)(2,1)S(1)} %shard_map.94), channel_id=1, source_target_pairs={{0,8},{4,12},{8,0},{12,4},{1,9},{5,13},{9,1},{13,5},{2,10},{6,14},... | collective-permute-start | bytes 221192 | tf_op jit(solution)/shard_map/ppermute | solution.py:926
  23.3 17.5 %collective-permute-start.8 = (bf16[1024,128]{1,0:T(8,128)(2,1)S(1)}, bf16[1024,128]{1,0:T(8,128)(2,1)S(1)}, u32[]{:S(2)}, u32[]{:S(2)}) collective-permute-start(bf16[1024,128]{1,0:T(8,128)(2,1)S(1)} %shard_map.100), channel_id=1, source_target_pairs={{0,8},{4,12},{8,0},{12,4},{1,9},{5,13},{9,1},{13,5},{2,10},{6,14},... | collective-permute-start | bytes 786440 | tf_op jit(solution)/shard_map/ppermute | solution.py:926
  28.5 13.2 %collective-permute-start.7 = (bf16[976,128]{1,0:T(8,128)(2,1)S(1)}, bf16[976,128]{1,0:T(8,128)(2,1)S(1)}, u32[]{:S(2)}, u32[]{:S(2)}) collective-permute-start(bf16[976,128]{1,0:T(8,128)(2,1)S(1)} %shard_map.99), channel_id=1, source_target_pairs={{0,8},{4,12},{8,0},{12,4},{1,9},{5,13},{9,1},{13,5},{2,10},{6,14},... | collective-permute-start | bytes 749576 | tf_op jit(solution)/shard_map/ppermute | solution.py:926
  29.0 2.6 %collective-permute-start.3 = (bf16[192,2,2,128]{3,0,1,2:T(8,128)(2,1)S(1)}, bf16[192,2,2,128]{3,0,1,2:T(8,128)(2,1)S(1)}, u32[]{:S(2)}, u32[]{:S(2)}) collective-permute-start(bf16[192,2,2,128]{3,0,1,2:T(8,128)(2,1)S(1)} %copy.38), channel_id=1, source_target_pairs={{0,4},{4,0},{8,12},{12,8},{1,5},{5,1},{9,13},{13,9},{2,6},{6,2},{1... | collective-permute-start | bytes 589832 | tf_op jit(solution)/shard_map/ppermute | solution.py:929
  30.6 4.6 %collective-permute-start.5 = (bf16[192,2,2,128]{3,0,1,2:T(8,128)(2,1)S(1)}, bf16[192,2,2,128]{3,0,1,2:T(8,128)(2,1)S(1)}, u32[]{:S(2)}, u32[]{:S(2)}) collective-permute-start(bf16[192,2,2,128]{3,0,1,2:T(8,128)(2,1)S(1)} %collective-permute-done.4), channel_id=1, source_target_pairs={{0,4},{4,0},{8,12},{12,8},{1,5},{5,1},{9,13},{13,9},{2,6},{6,2},{1... | collective-permute-start | bytes 589832 | tf_op jit(solution)/shard_map/ppermute | solution.py:929
